TPU v7x, 32 devices: a whole 2x2x4 slice. The times are simulated.
32 devices in a mesh: dp: 8 (over z, y), zero: 4 (over x, core).
Axes of the slice: x: 2, y: 2, z: 4, core: 2. Of those that a mesh axis runs over, the one named last changes fastest.
Arguments:
- tokens: bfloat16 [8, 512, 768], P('dp', 'zero'), may hold values from -6 to 6
- cotangent: bfloat16 [8, 512, 768], P('dp', 'zero'), may hold values from -6 to 6
- params: float32 [4, 8, 156720], P('zero', 'dp'), may hold values from -2 to 2
- first_moment: float32 [4, 8, 156720], P('zero', 'dp'), may hold values from -0.15625 to 0.15625
- second_moment: float32 [4, 8, 156720], P('zero', 'dp'), may hold values from 0.005 to 0.05
Outputs:
- output: bfloat16 [8, 512, 768], P('dp', 'zero')
- grad_tokens: float32 [8, 512, 768], P('dp', 'zero')
- grad_params: float32 [4, 8, 156720], P('zero', 'dp')
- new_params: float32 [4, 8, 156720], P('zero', 'dp')
- new_first: float32 [4, 8, 156720], P('zero', 'dp')
- new_second: float32 [4, 8, 156720], P('zero', 'dp')
All inputs are finite; a program needn't handle non-finite values.
Results may differ from a plain program's by a relative error of at most 0.019.
Values may be sent and summed in bfloat16 or wider, within the bound.
A program may use at most 128 MiB of HBM per device.

v0:
```python
import math

import jax
import jax.numpy as jnp
from jax import lax
from jax.sharding import PartitionSpec as P

D = 768
FF = 1152
HEAD = 64
HALF_WIN = 64
STEP = 3


norm_eps = 1e-05
beta_one = 0.9
beta_two = 0.98
adam_eps = 1e-06
rope_base = 10000.0
matrix_rate = 0.01
matrix_decay = 0.1
gain_rate = 0.1
masked_score = -1e30


def norm_forward(values):
    centred = values - jnp.mean(values, axis=-1, keepdims=True)
    inverse = lax.rsqrt(jnp.mean(centred * centred, axis=-1, keepdims=True) + norm_eps)
    return (centred * inverse, inverse)


def norm_backward(grad_norm, gain_vec, normed, inverse):
    scaled = grad_norm * gain_vec
    return inverse * (
        scaled
        - jnp.mean(scaled, axis=-1, keepdims=True)
        - normed * jnp.mean(scaled * normed, axis=-1, keepdims=True)
    )


def rotary_tables(length):
    position = lax.iota(jnp.float32, length)
    exponent = lax.iota(jnp.float32, HEAD // 2) * (2.0 / HEAD)
    inv_freq = jnp.exp(-math.log(rope_base) * exponent)
    phases = position[:, None] * inv_freq[None, :]
    cosine = jnp.concatenate([jnp.cos(phases), jnp.cos(phases)], axis=-1)[:, None, :]
    sine_table = jnp.concatenate([jnp.sin(phases), jnp.sin(phases)], axis=-1)[:, None, :]
    return (cosine, sine_table)


def rotate_half(values):
    middle = values.shape[-1] // 2
    return jnp.concatenate([-values[..., middle:], values[..., :middle]], axis=-1)


def rotate_back(values):
    middle = values.shape[-1] // 2
    return jnp.concatenate([values[..., middle:], -values[..., :middle]], axis=-1)


def gelu_parts(values):
    cdf_part = 0.5 * (1.0 + jax.scipy.special.erf(values * (1.0 / math.sqrt(2.0))))
    pdf_part = jnp.exp(-0.5 * values * values) * (1.0 / math.sqrt(2.0 * math.pi))
    return (values * cdf_part, cdf_part + values * pdf_part)


def window_keys(values, block_rows):
    seq_count, length = (values.shape[0], values.shape[1])
    padded = jnp.pad(values, ((0, 0), (block_rows // 2, block_rows // 2), (0, 0), (0, 0)))
    blocks = padded.reshape(
        seq_count, length // block_rows + 1, block_rows, values.shape[2], values.shape[3]
    )
    return jnp.concatenate([blocks[:, :-1], blocks[:, 1:]], axis=2)


def fold_keys(windows, block_rows):
    seq_count, block_count = (windows.shape[0], windows.shape[1])
    zeros_block = jnp.zeros_like(windows[:, :1, :block_rows])
    low_part = jnp.concatenate([windows[:, :, :block_rows], zeros_block], axis=1)
    high_part = jnp.concatenate([zeros_block, windows[:, :, block_rows:]], axis=1)
    merged = (low_part + high_part).reshape(
        seq_count, (block_count + 1) * block_rows, windows.shape[3], windows.shape[4]
    )
    return merged[:, block_rows // 2 : block_rows // 2 + block_count * block_rows]


def band_mask(length, block_rows):
    block_count = length // block_rows
    dims = (block_count, block_rows, 2 * block_rows)
    query_pos = lax.broadcasted_iota(jnp.int32, dims, 1)
    key_pos = lax.broadcasted_iota(jnp.int32, dims, 2)
    block_pos = lax.broadcasted_iota(jnp.int32, dims, 0)
    relative = key_pos - query_pos
    absolute = block_pos * block_rows - block_rows // 2 + key_pos
    return (relative >= 0) & (relative <= block_rows) & (absolute >= 0) & (absolute < length)


def per_device(tokens, cotangent, params, first_moment, second_moment):
    zero_count = lax.axis_size("zero")
    dp_count = lax.axis_size("dp")
    shard_size = params.shape[2]
    quarter = D // zero_count
    ff_part = FF // zero_count
    ffn_piece = 3 * D * FF // zero_count // dp_count
    attn_piece = shard_size - ffn_piece
    own_bf = params.astype(jnp.bfloat16)
    slice_all = lax.all_gather(own_bf, "dp", axis=1, tiled=True).reshape(dp_count, shard_size)
    ffn_flat = slice_all[:, :ffn_piece].reshape(-1)
    attn_flat = slice_all[:, ffn_piece:].reshape(-1)
    first_end = 3 * quarter * D
    second_end = first_end + D * quarter
    w_qkv = attn_flat[:first_end].reshape(3 * quarter, D)
    w_attn = attn_flat[first_end:second_end].reshape(D, quarter)
    gains = lax.all_gather(attn_flat[second_end:].reshape(2, quarter), "zero", axis=1, tiled=True)
    gain_one32 = gains[0].astype(jnp.float32)
    gain_two32 = gains[1].astype(jnp.float32)
    lift_end = 2 * ff_part * D
    w_input = ffn_flat[:lift_end].reshape(2 * ff_part, D)
    w_output = ffn_flat[lift_end:].reshape(D, ff_part)
    seq_count, own_len = (tokens.shape[0], tokens.shape[1])
    own_rows = seq_count * own_len
    length = own_len * zero_count
    row_count = seq_count * length
    local_heads = quarter // HEAD
    block_rows = 2 * HALF_WIN
    block_count = length // block_rows
    cosine, sine_table = rotary_tables(length)
    allowed = band_mask(length, block_rows)[None, :, None]
    inputs = tokens.astype(jnp.float32).reshape(own_rows, D)
    normed_one, inverse_one = norm_forward(inputs)
    normal_one = (normed_one * gain_one32).astype(jnp.bfloat16).reshape(seq_count, own_len, D)
    full_one = lax.all_gather(normal_one, "zero", axis=1, tiled=True).reshape(row_count, D)
    projected = jnp.dot(full_one, w_qkv.T, preferred_element_type=jnp.float32)
    projected = projected.reshape(seq_count, length, 3, local_heads, HEAD)
    queries = (projected[:, :, 0] * cosine + rotate_half(projected[:, :, 0]) * sine_table).astype(
        jnp.bfloat16
    )
    key_rows = (projected[:, :, 1] * cosine + rotate_half(projected[:, :, 1]) * sine_table).astype(
        jnp.bfloat16
    )
    value_rows = projected[:, :, 2].astype(jnp.bfloat16)
    query_blocks = queries.reshape(seq_count, block_count, block_rows, local_heads, HEAD)
    key_windows = window_keys(key_rows, block_rows)
    value_windows = window_keys(value_rows, block_rows)
    scores = (
        jnp.einsum(
            "sbqhe,sbkhe->sbhqk", query_blocks, key_windows, preferred_element_type=jnp.float32
        )
        * 0.125
    )
    scores = jnp.where(allowed, scores, masked_score)
    row_max = jnp.max(scores, axis=-1, keepdims=True)
    log_total = row_max + jnp.log(jnp.sum(jnp.exp(scores - row_max), axis=-1, keepdims=True))
    attn_probs = jnp.exp(scores - log_total).astype(jnp.bfloat16)
    context = jnp.einsum(
        "sbhqk,sbkhe->sbqhe", attn_probs, value_windows, preferred_element_type=jnp.float32
    ).astype(jnp.bfloat16)
    context_rows = context.reshape(row_count, quarter)
    attn_terms = jnp.dot(context_rows, w_attn.T, preferred_element_type=jnp.float32)
    attn_sum = lax.psum_scatter(
        attn_terms.reshape(seq_count, length, D).astype(jnp.bfloat16),
        "zero",
        scatter_dimension=1,
        tiled=True,
    ).astype(jnp.float32)
    hidden = inputs + attn_sum.reshape(own_rows, D)
    normed_two, inverse_two = norm_forward(hidden)
    normal_two = (normed_two * gain_two32).astype(jnp.bfloat16).reshape(seq_count, own_len, D)
    full_two = lax.all_gather(normal_two, "zero", axis=1, tiled=True).reshape(row_count, D)
    lifted = jnp.dot(full_two, w_input.T, preferred_element_type=jnp.float32)
    gate_act, gate_slope = gelu_parts(lifted[:, :ff_part])
    up_half = lifted[:, ff_part:]
    mixed = (gate_act * up_half).astype(jnp.bfloat16)
    ffn_terms = jnp.dot(mixed, w_output.T, preferred_element_type=jnp.float32)
    ffn_sum = lax.psum_scatter(
        ffn_terms.reshape(seq_count, length, D).astype(jnp.bfloat16),
        "zero",
        scatter_dimension=1,
        tiled=True,
    ).astype(jnp.float32)
    output = hidden + ffn_sum.reshape(own_rows, D)
    grad_scale = float(dp_count * row_count) ** (-0.5)
    cot_full = lax.all_gather(cotangent, "zero", axis=1, tiled=True).reshape(row_count, D)
    grad_output_w = jnp.dot(cot_full.T, mixed, preferred_element_type=jnp.float32)
    grad_mixed = jnp.dot(cot_full, w_output, preferred_element_type=jnp.float32)
    grad_lifted = jnp.concatenate(
        [grad_mixed * up_half * gate_slope, grad_mixed * gate_act], axis=-1
    ).astype(jnp.bfloat16)
    grad_input_w = jnp.dot(grad_lifted.T, full_two, preferred_element_type=jnp.float32)
    ffn_vec = jnp.concatenate([grad_input_w.ravel(), grad_output_w.ravel()]) * grad_scale
    ffn_vec = ffn_vec.reshape(dp_count, ffn_piece)
    norm_two_terms = jnp.dot(grad_lifted, w_input, preferred_element_type=jnp.float32)
    grad_norm_two = (
        lax.psum_scatter(
            norm_two_terms.reshape(seq_count, length, D).astype(jnp.bfloat16),
            "zero",
            scatter_dimension=1,
            tiled=True,
        )
        .astype(jnp.float32)
        .reshape(own_rows, D)
    )
    gain_two_term = jnp.sum(grad_norm_two * normed_two, axis=0)
    grad_hidden = cotangent.reshape(own_rows, D).astype(jnp.float32) + norm_backward(
        grad_norm_two, gain_two32, normed_two, inverse_two
    )
    grad_hidden_b = grad_hidden.astype(jnp.bfloat16).reshape(seq_count, own_len, D)
    hidden_full = lax.all_gather(grad_hidden_b, "zero", axis=1, tiled=True).reshape(row_count, D)
    grad_attn_w = jnp.dot(hidden_full.T, context_rows, preferred_element_type=jnp.float32)
    grad_context = jnp.dot(hidden_full, w_attn, preferred_element_type=jnp.float32).astype(
        jnp.bfloat16
    )
    grad_context = grad_context.reshape(seq_count, block_count, block_rows, local_heads, HEAD)
    again = (
        jnp.einsum(
            "sbqhe,sbkhe->sbhqk", query_blocks, key_windows, preferred_element_type=jnp.float32
        )
        * 0.125
    )
    probs_full = jnp.exp(jnp.where(allowed, again, masked_score) - log_total)
    grad_probs = jnp.einsum(
        "sbqhe,sbkhe->sbhqk", grad_context, value_windows, preferred_element_type=jnp.float32
    )
    row_term = jnp.sum(grad_context.astype(jnp.float32) * context.astype(jnp.float32), axis=-1)
    row_term = jnp.transpose(row_term, (0, 1, 3, 2))[..., None]
    grad_scores = (probs_full * (grad_probs - row_term) * 0.125).astype(jnp.bfloat16)
    probs_b = probs_full.astype(jnp.bfloat16)
    grad_query = jnp.einsum(
        "sbhqk,sbkhe->sbqhe", grad_scores, key_windows, preferred_element_type=jnp.float32
    ).reshape(seq_count, length, local_heads, HEAD)
    grad_key = fold_keys(
        jnp.einsum(
            "sbhqk,sbqhe->sbkhe", grad_scores, query_blocks, preferred_element_type=jnp.float32
        ),
        block_rows,
    )
    grad_value = fold_keys(
        jnp.einsum("sbhqk,sbqhe->sbkhe", probs_b, grad_context, preferred_element_type=jnp.float32),
        block_rows,
    )
    grad_query = grad_query * cosine + rotate_back(grad_query * sine_table)
    grad_key = grad_key * cosine + rotate_back(grad_key * sine_table)
    grad_packed = (
        jnp.stack([grad_query, grad_key, grad_value], axis=2)
        .astype(jnp.bfloat16)
        .reshape(row_count, 3 * quarter)
    )
    grad_qkv_w = jnp.dot(grad_packed.T, full_one, preferred_element_type=jnp.float32)
    norm_one_terms = jnp.dot(grad_packed, w_qkv, preferred_element_type=jnp.float32)
    grad_norm_one = (
        lax.psum_scatter(
            norm_one_terms.reshape(seq_count, length, D).astype(jnp.bfloat16),
            "zero",
            scatter_dimension=1,
            tiled=True,
        )
        .astype(jnp.float32)
        .reshape(own_rows, D)
    )
    gain_one_term = jnp.sum(grad_norm_one * normed_one, axis=0)
    grad_inputs = grad_hidden + norm_backward(grad_norm_one, gain_one32, normed_one, inverse_one)
    gain_grads = lax.psum_scatter(
        jnp.stack([gain_one_term, gain_two_term]), "zero", scatter_dimension=1, tiled=True
    )
    attn_vec = (
        jnp.concatenate([grad_qkv_w.ravel(), grad_attn_w.ravel(), gain_grads.ravel()]) * grad_scale
    )
    attn_vec = attn_vec.reshape(dp_count, attn_piece)
    grad_shard = lax.psum_scatter(
        jnp.concatenate([ffn_vec, attn_vec], axis=1), "dp", scatter_dimension=0, tiled=True
    )
    grad_shard = grad_shard.reshape(params.shape)
    new_first = beta_one * first_moment + (1.0 - beta_one) * grad_shard
    new_second = beta_two * second_moment + (1.0 - beta_two) * grad_shard * grad_shard
    first_hat = new_first / (1.0 - beta_one**STEP)
    second_hat = new_second / (1.0 - beta_two**STEP)
    attn_total = attn_piece * dp_count
    place = lax.axis_index("dp") * attn_piece + lax.iota(jnp.int32, attn_piece)
    gain_tail = place >= attn_total - 2 * quarter
    gain_part = jnp.concatenate([jnp.zeros((ffn_piece,), jnp.bool_), gain_tail]).reshape(
        params.shape
    )
    step_rate = jnp.where(gain_part, gain_rate, matrix_rate)
    decay_rate = jnp.where(gain_part, 0.0, matrix_decay)
    direction = first_hat / (jnp.sqrt(second_hat) + adam_eps)
    new_params = params - step_rate * (direction + decay_rate * params)
    return (
        output.astype(jnp.bfloat16).reshape(tokens.shape),
        grad_inputs.reshape(tokens.shape),
        grad_shard,
        new_params,
        new_first,
        new_second,
    )


def solution(mesh):
    in_specs = (
        P("dp", "zero", None),
        P("dp", "zero", None),
        P("zero", "dp", None),
        P("zero", "dp", None),
        P("zero", "dp", None),
    )
    out_specs = (
        P("dp", "zero", None),
        P("dp", "zero", None),
        P("zero", "dp", None),
        P("zero", "dp", None),
        P("zero", "dp", None),
        P("zero", "dp", None),
    )
    return jax.shard_map(
        per_device, mesh=mesh, in_specs=in_specs, out_specs=out_specs, check_vma=False
    )
```

profile of v0, /device:TPU:0, one launch (start us, length us, event | category | flops | bytes accessed | tf_op | source)
XLA Modules:
  0.0 489.6 jit_solution(632954741733930993)
XLA Ops:
  7.2 2.2 bitcast_convert_fusion
  12.0 84.5 %all-gather.3.cloned.1.call-done = bf16[1,8,156720]{2,0,1:T(2,128)(2,1)} async-done(((bf16[1,1,156720]{2,0,1:T(2,128)(2,1)}), bf16[1,8,156720]{2,0,1:T(2,128)(2,1)}) %all-gather.3.cloned.1.call-update) | async-done | bytes 2507536 | tf_op jit(solution)/shard_map/all_gather | solution.py:107
  96.6 4.2 copy.115
  103.6 2.2 slice.111
  107.3 5.1 %all-gather = bf16[4,192,2]{1,2,0:T(2,128)(2,1)S(1)} all-gather(bf16[1,192,2]{1,2,0:T(2,128)(2,1)S(1)} %slice_bitcast_fusion.3), channel_id=1, replica_groups=mesh['dp'=8,'zero'=4] {'zero'}, dimensions={0}, use_global_device_ids=true | all-gather | bytes 3840 | tf_op jit(solution)/shard_map/all_gather | solution.py:114
  113.1 8.7 %all_gather.20 = bf16[1,512,768]{2,1,0:T(8,128)(2,1)S(1)} all-gather(bf16[1,128,768]{2,1,0:T(8,128)(2,1)S(1)} %fusion.65), channel_id=1, replica_groups=mesh['dp'=8,'zero'=4] {'zero'}, dimensions={1}, use_global_device_ids=true | all-gather | bytes 983040 | tf_op jit(solution)/shard_map/all_gather | solution.py:132
  130.9 2.3 fusion.4
  133.3 9.3 %all_gather.22 = bf16[1,512,768]{2,1,0:T(8,128)(2,1)} all-gather(bf16[1,128,768]{2,1,0:T(8,128)(2,1)S(1)} %copy-done.20), channel_id=1, replica_groups=mesh['dp'=8,'zero'=4] {'zero'}, dimensions={1}, use_global_device_ids=true | all-gather | bytes 983040 | tf_op jit(solution)/shard_map/all_gather | solution.py:183
  144.1 3.1 slice.129
  148.8 4.6 slice.133
  158.1 8.0 %all_gather.21 = bf16[1,512,768]{2,1,0:T(8,128)(2,1)S(1)} all-gather(bf16[1,128,768]{2,1,0:T(8,128)(2,1)S(1)} %multiply_convert_fusion.3), channel_id=1, replica_groups=mesh['dp'=8,'zero'=4] {'zero'}, dimensions={1}, use_global_device_ids=true | all-gather | bytes 983040 | tf_op jit(solution)/shard_map/all_gather | solution.py:169
  168.2 2.5 fusion.29
  171.6 1.7 fusion.2
  173.3 1.7 reshape.789
  175.0 2.3 convolution_bitcast_fusion.1
  178.9 1.8 reshape.792
  180.6 2.0 fusion.13
  184.0 13.2 %reduce-scatter.12.cloned.1.call-done = bf16[1,128,768]{2,1,0:T(8,128)(2,1)} async-done(((bf16[1,512,768]{2,1,0:T(8,128)(2,1)}), bf16[1,128,768]{2,1,0:T(8,128)(2,1)}) %reduce-scatter.12.cloned.1.call-update) | async-done | bytes 196624 | tf_op jit(solution)/shard_map/reduce_scatter | solution.py:194
  199.9 8.3 %all_gather.23 = bf16[1,512,768]{2,1,0:T(8,128)(2,1)S(1)} all-gather(bf16[1,128,768]{2,1,0:T(8,128)(2,1)S(1)} %fusion.101), channel_id=1, replica_groups=mesh['dp'=8,'zero'=4] {'zero'}, dimensions={1}, use_global_device_ids=true | all-gather | bytes 983040 | tf_op jit(solution)/shard_map/all_gather | solution.py:208
  217.2 1.7 fusion.3
  219.0 1.9 maximum_multiply_fusion
  220.9 21.9 %reduce-scatter.14.cloned.1.call-done = bf16[1,128,768]{2,1,0:T(8,128)(2,1)} async-done(((bf16[1,512,768]{2,1,0:T(8,128)(2,1)}), bf16[1,128,768]{2,1,0:T(8,128)(2,1)}) %reduce-scatter.14.cloned.1.call-update) | async-done | bytes 196624 | tf_op jit(solution)/shard_map/reduce_scatter | solution.py:251
  245.0 2.6 fusion.1
  247.7 1.9 mul.580
  251.5 1.8 fusion.17
  255.2 11.3 %reduce-scatter.16.cloned.1.call-done = f32[192,2]{1,0:T(8,128)} async-done(((f32[768,2]{1,0:T(8,128)}), f32[192,2]{1,0:T(8,128)}) %reduce-scatter.16.cloned.1.call-update) | async-done | bytes 1552
  269.2 4.5 mul.585
  273.7 4.6 pad_maximum_fusion
  279.8 12.4 %reduce-scatter.10.cloned.1.call-done = bf16[1,128,768]{2,1,0:T(8,128)(2,1)} async-done(((bf16[1,512,768]{2,1,0:T(8,128)(2,1)}), bf16[1,128,768]{2,1,0:T(8,128)(2,1)}) %reduce-scatter.10.cloned.1.call-update) | async-done | bytes 196624 | tf_op jit(solution)/shard_map/reduce_scatter | solution.py:175
  292.2 2.1 fusion.61
  294.3 180.0 %all-reduce.10.cloned.1.call-done = f32[8,156720]{1,0:T(8,128)} async-done(((f32[8,156720]{1,0:T(8,128)}), f32[8,156720]{1,0:T(8,128)}) %all-reduce.10.cloned.1.call-update) | async-done | bytes 5015056
  474.3 8.4 %multiply_subtract_fusion = (f32[1,1,156720]{2,1,0:T(1,128)}, f32[1,1,156720]{2,1,0:T(1,128)}, f32[1,1,156720]{2,1,0:T(1,128)}, f32[1,1,156720]{2,1,0:T(1,128)}) fusion(f32[1,1,156720]{2,1,0:T(1,128)S(1)} %copy-done.13, f32[156720]{0:T(1024)S(1)} %get-tuple-element.45, f32[156720]{0:T(1024)S(1)} %get-tuple-element.44, f32[1,1,156720]{2,1,0:T(1,128)S(1)} %copy-done.37, ...), kind=kLoop, calls=%fused_computation.54 | loop fusion | flops 2350800 | bytes 6268804 | tf_op jit(solution)/shard_map/sub | solution.py:286
  (223 shorter events, 51.7 us)
Async XLA Ops:
  7.2 3.7 copy-start
  7.2 89.4 %all-gather.3.cloned.1.call-start = ((), (), s32[]{:S(2)}) async-start(), calls=%async_computation.5 | async-start | bytes 5644800 | tf_op jit(solution)/shard_map/all_gather | solution.py:107
  9.4 145.5 %reduce-scatter.8.cloned.1.call-start = ((), (), s32[]{:S(2)}) async-start(), calls=%async_computation.6 | async-start | bytes 983040 | tf_op jit(solution)/shard_map/reduce_scatter | solution.py:160
  10.9 114.5 %copy-start.14 = (f32[512,64]{0,1:T(8,128)}, f32[512,64]{0,1:T(8,128)S(1)}, u32[]{:S(2)}) copy-start(f32[512,64]{0,1:T(8,128)S(1)} %get-tuple-element.56) | copy-start | bytes 393220
  10.9 114.5 %copy-start.22 = (f32[512,64]{0,1:T(8,128)}, f32[512,64]{0,1:T(8,128)S(1)}, u32[]{:S(2)}) copy-start(f32[512,64]{0,1:T(8,128)S(1)} %get-tuple-element.57) | copy-start | bytes 393220
  11.0 101.5 %copy-start.44 = (f32[128]{0:T(128)}, f32[128]{0:T(128)S(1)}, u32[]{:S(2)}) copy-start(f32[128]{0:T(128)S(1)} %broadcast_multiply_fusion.5) | copy-start | bytes 1540
  11.2 101.3 %copy-start.48 = (f32[128]{0:T(128)}, f32[128]{0:T(128)S(1)}, u32[]{:S(2)}) copy-start(f32[128]{0:T(128)S(1)} %add_rsqrt_fusion.1) | copy-start | bytes 1540
  103.6 3.0 copy-start.2
  130.1 3.2 copy-start.20
  133.3 63.9 %reduce-scatter.12.cloned.1.call-start = ((), (), s32[]{:S(2)}) async-start(), calls=%async_computation.8 | async-start | bytes 983040 | tf_op jit(solution)/shard_map/reduce_scatter | solution.py:194
  153.4 13.6 %copy-start.9 = (bf16[864,768]{1,0:T(8,128)(2,1)S(1)}, bf16[864,768]{1,0:T(8,128)(2,1)}, u32[]{:S(2)}) copy-start(bf16[864,768]{1,0:T(8,128)(2,1)} %slice.129) | copy-start | bytes 3981316
  157.1 10.7 %copy-start.46 = (f32[128]{0:T(128)}, f32[128]{0:T(128)S(1)}, u32[]{:S(2)}) copy-start(f32[128]{0:T(128)S(1)} %add_rsqrt_fusion) | copy-start | bytes 1540
  168.2 3.3 copy-start.10
  173.3 69.5 %reduce-scatter.14.cloned.1.call-start = ((), (), s32[]{:S(2)}) async-start(), calls=%async_computation.9 | async-start | bytes 983040 | tf_op jit(solution)/shard_map/reduce_scatter | solution.py:251
  198.5 11.9 %copy-start.50 = (f32[128]{0:T(128)}, f32[128]{0:T(128)S(1)}, u32[]{:S(2)}) copy-start(f32[128]{0:T(128)S(1)} %broadcast_multiply_fusion.2) | copy-start | bytes 1540
  198.5 11.9 %copy-start.52 = (f32[128]{0:T(128)}, f32[128]{0:T(128)S(1)}, u32[]{:S(2)}) copy-start(f32[128]{0:T(128)S(1)} %broadcast_multiply_fusion.3) | copy-start | bytes 1540
  218.9 23.9 %copy-start.43 = (f32[768]{0:T(1024)S(1)}, f32[768]{0:T(1024)}, u32[]{:S(2)}) copy-start(f32[768]{0:T(1024)} %copy-done.42) | copy-start | bytes 9220
  218.9 23.9 %copy-start.45 = (f32[128]{0:T(128)S(1)}, f32[128]{0:T(128)}, u32[]{:S(2)}) copy-start(f32[128]{0:T(128)} %copy-done.44) | copy-start | bytes 1540
  218.9 23.9 %copy-start.49 = (f32[128]{0:T(128)S(1)}, f32[128]{0:T(128)}, u32[]{:S(2)}) copy-start(f32[128]{0:T(128)} %copy-done.48) | copy-start | bytes 1540
  218.9 47.6 %reduce-scatter.16.cloned.1.call-start = ((), (), s32[]{:S(2)}) async-start(), calls=%async_computation.10 | async-start | bytes 491520
  245.0 47.2 %reduce-scatter.10.cloned.1.call-start = ((), (), s32[]{:S(2)}) async-start(), calls=%async_computation.7 | async-start | bytes 983040 | tf_op jit(solution)/shard_map/reduce_scatter | solution.py:175
  249.6 224.7 %all-reduce.10.cloned.1.call-start = ((), (), s32[]{:S(2)}) async-start(), calls=%async_computation.11 | async-start | bytes 10035200
  269.2 4.5 copy-start.1
  278.3 13.9 %copy-start.47 = (f32[128]{0:T(128)S(1)}, f32[128]{0:T(128)}, u32[]{:S(2)}) copy-start(f32[128]{0:T(128)} %copy-done.46) | copy-start | bytes 1540
  278.3 13.9 %copy-start.51 = (f32[128]{0:T(128)S(1)}, f32[128]{0:T(128)}, u32[]{:S(2)}) copy-start(f32[128]{0:T(128)} %copy-done.50) | copy-start | bytes 1540
  278.3 13.9 %copy-start.53 = (f32[128]{0:T(128)S(1)}, f32[128]{0:T(128)}, u32[]{:S(2)}) copy-start(f32[128]{0:T(128)} %copy-done.52) | copy-start | bytes 1540
  278.4 13.8 %copy-start.8 = (bf16[1,128,768]{2,1,0:T(8,128)(2,1)S(1)}, bf16[1,128,768]{2,1,0:T(8,128)(2,1)}, u32[]{:S(2)}) copy-start(bf16[1,128,768]{2,1,0:T(8,128)(2,1)} %reduce-scatter.8.cloned.1.call-done) | copy-start | bytes 589828
  278.4 13.8 %copy-start.18 = (bf16[1,128,768]{2,1,0:T(8,128)(2,1)S(1)}, bf16[1,128,768]{2,1,0:T(8,128)(2,1)}, u32[]{:S(2)}) copy-start(bf16[1,128,768]{2,1,0:T(8,128)(2,1)} %reduce-scatter.12.cloned.1.call-done) | copy-start | bytes 589828
  278.4 13.8 %copy-start.21 = (bf16[1,128,768]{2,1,0:T(8,128)(2,1)S(1)}, bf16[1,128,768]{2,1,0:T(8,128)(2,1)}, u32[]{:S(2)}) copy-start(bf16[1,128,768]{2,1,0:T(8,128)(2,1)} %param.6) | copy-start | bytes 589828
  278.4 13.8 %copy-start.27 = (bf16[1,128,768]{2,1,0:T(8,128)(2,1)S(1)}, bf16[1,128,768]{2,1,0:T(8,128)(2,1)}, u32[]{:S(2)}) copy-start(bf16[1,128,768]{2,1,0:T(8,128)(2,1)} %reduce-scatter.14.cloned.1.call-done) | copy-start | bytes 589828
  279.7 194.6 %copy-start.13 = (f32[1,1,156720]{2,1,0:T(1,128)S(1)}, f32[1,1,156720]{2,1,0:T(1,128)}, u32[]{:S(2)}) copy-start(f32[1,1,156720]{2,1,0:T(1,128)} %param.7) | copy-start | bytes 1880644
  279.7 194.6 %copy-start.37 = (f32[1,1,156720]{2,1,0:T(1,128)S(1)}, f32[1,1,156720]{2,1,0:T(1,128)}, u32[]{:S(2)}) copy-start(f32[1,1,156720]{2,1,0:T(1,128)} %param.8) | copy-start | bytes 1880644
  (30 other events, 32.2 us)
Sparse Core Ops, SparseCore 0:
  10.8 85.7 all-gather.2
  133.4 21.4 reduce-scatter.7
  173.4 23.7 reduce-scatter.11
  219.0 23.7 reduce-scatter.13
  245.7 20.7 reduce-scatter.15
  268.9 23.2 reduce-scatter.9
  295.9 178.3 all-reduce.9
where the time goes:
time: 491 us; the launch traced here: 490 us
  waiting for transfers between devices  325 us (66%)
  local copies, waits for them, and re-layouts  52.7 us (11%)
  blocking collectives  39.4 us (8%)
  other arithmetic  32.9 us (7%)
  matrix products  24.1 us (5%)
  between operations  15.1 us (3%)
    unnamed x9, waiting for transfers between devices  191 us
    all_gather x1, waiting for transfers between devices, per_device(): lax.all_gather(own_bf, 'dp', axis=1, tiled=True)  84.5 us
    reduce_scatter x1, waiting for transfers between devices, per_device(): lax.psum_scatter(norm_one_terms.reshape(seq_count, length, D).astype(jnp....  21.9 us
    unnamed x122, local copies, waits for them, and re-layouts  20.3 us
    reduce_scatter x1, waiting for transfers between devices, per_device(): lax.psum_scatter(norm_two_terms.reshape(seq_count, length, D).astype(jnp....  13.2 us
    reduce_scatter x1, waiting for transfers between devices, per_device(): lax.psum_scatter(ffn_terms.reshape(seq_count, length, D).astype(jnp.bfloa...  12.4 us
  transfers between devices with their start and end apart: 7, of which 7 were waited for; matrix products, arithmetic and copies ran while one was open for 10% of the time, Pallas kernels for 0%

commit v1 on v0

--- a/solution.py
+++ b/solution.py
@@ -3,6 +3,8 @@
 import jax
 import jax.numpy as jnp
 from jax import lax
+from jax.experimental import pallas as pl
+from jax.experimental.pallas import tpu as pltpu
 from jax.sharding import PartitionSpec as P
 
 D = 768
@@ -95,6 +97,314 @@
     return (relative >= 0) & (relative <= block_rows) & (absolute >= 0) & (absolute < length)
 
 
+MESH = pl.DeviceIdType.MESH
+VM = pl.BlockSpec(memory_space=pltpu.VMEM)
+PIECES = 4
+
+
+def remote(src, dst, send_sem, recv_sem, axis, index):
+    return pltpu.make_async_remote_copy(
+        src_ref=src,
+        dst_ref=dst,
+        send_sem=send_sem,
+        recv_sem=recv_sem,
+        device_id={axis: index},
+        device_id_type=MESH,
+    )
+
+
+def greet(targets):
+    barrier = pltpu.get_barrier_semaphore()
+    for axis, index in targets:
+        pl.semaphore_signal(barrier, inc=1, device_id={axis: index}, device_id_type=MESH)
+    pl.semaphore_wait(barrier, len(targets))
+
+
+def zero_places():
+    me = lax.axis_index("zero")
+    chip, core = me // 2, me % 2
+    mate = chip * 2 + 1 - core
+    across = (1 - chip) * 2 + core
+    diagonal = (1 - chip) * 2 + 1 - core
+    return me, mate, across, diagonal
+
+
+def zero_gather_kernel(x_ref, out_ref, own_sem, send_sem, recv_sem, far_send, far_recv, fwd_send, fwd_recv):
+    me, mate, across, diagonal = zero_places()
+    rows = x_ref.shape[0]
+    part = rows // PIECES
+    greet([("zero", mate), ("zero", across)])
+    far, fwd = [], []
+    for k in range(PIECES):
+        copy = remote(
+            x_ref.at[pl.ds(k * part, part)],
+            out_ref.at[me, pl.ds(k * part, part)],
+            far_send.at[k],
+            far_recv.at[k],
+            "zero",
+            across,
+        )
+        copy.start()
+        far.append(copy)
+    near = remote(x_ref, out_ref.at[me], send_sem, recv_sem, "zero", mate)
+    near.start()
+    own = pltpu.make_async_copy(x_ref, out_ref.at[me], own_sem)
+    own.start()
+    for k in range(PIECES):
+        far[k].wait_recv()
+        piece = out_ref.at[across, pl.ds(k * part, part)]
+        copy = remote(piece, piece, fwd_send.at[k], fwd_recv.at[k], "zero", mate)
+        copy.start()
+        fwd.append(copy)
+    own.wait()
+    near.wait()
+    for k in range(PIECES):
+        far[k].wait_send()
+        fwd[k].wait()
+
+
+def zero_gather(x, collective_id):
+    zero_count = lax.axis_size("zero")
+    rows, width = x.shape
+    out = pl.pallas_call(
+        zero_gather_kernel,
+        out_shape=jax.ShapeDtypeStruct((zero_count, rows, width), x.dtype),
+        in_specs=[VM],
+        out_specs=VM,
+        scratch_shapes=[pltpu.SemaphoreType.DMA] * 3 + [pltpu.SemaphoreType.DMA((PIECES,))] * 4,
+        compiler_params=pltpu.CompilerParams(collective_id=collective_id, has_side_effects=True),
+    )(x)
+    return out.reshape(zero_count * rows, width)
+
+
+def zero_scatter_kernel(
+    terms_ref, out_ref, mine, mixed, total, far, mate_send, mate_recv, mix_send, mix_recv, far_send, far_recv
+):
+    me, mate, across, diagonal = zero_places()
+    rows = terms_ref.shape[1]
+    part = rows // PIECES
+    greet([("zero", mate), ("zero", across)])
+    mixes, fars = [], []
+    for k in range(PIECES):
+        copy = remote(
+            terms_ref.at[diagonal, pl.ds(k * part, part)],
+            mixed.at[pl.ds(k * part, part)],
+            mix_send.at[k],
+            mix_recv.at[k],
+            "zero",
+            mate,
+        )
+        copy.start()
+        mixes.append(copy)
+    near = remote(terms_ref.at[mate], mine, mate_send, mate_recv, "zero", mate)
+    near.start()
+    for k in range(PIECES):
+        mixes[k].wait_recv()
+        piece = pl.ds(k * part, part)
+        total[piece] = (
+            terms_ref[across, piece].astype(jnp.float32) + mixed[piece].astype(jnp.float32)
+        ).astype(jnp.bfloat16)
+        copy = remote(
+            total.at[piece], far.at[piece], far_send.at[k], far_recv.at[k], "zero", across
+        )
+        copy.start()
+        fars.append(copy)
+    near.wait()
+    for k in range(PIECES):
+        piece = pl.ds(k * part, part)
+        fars[k].wait_recv()
+        out_ref[piece] = (
+            terms_ref[me, piece].astype(jnp.float32)
+            + mine[piece].astype(jnp.float32)
+            + far[piece].astype(jnp.float32)
+        )
+    for k in range(PIECES):
+        mixes[k].wait_send()
+        fars[k].wait_send()
+
+
+def zero_scatter(terms, collective_id):
+    zero_count = lax.axis_size("zero")
+    rows, width = terms.shape[0] // zero_count, terms.shape[1]
+    buf = pltpu.VMEM((rows, width), jnp.bfloat16)
+    return pl.pallas_call(
+        zero_scatter_kernel,
+        out_shape=jax.ShapeDtypeStruct((rows, width), jnp.float32),
+        in_specs=[VM],
+        out_specs=VM,
+        scratch_shapes=[buf] * 4
+        + [pltpu.SemaphoreType.DMA] * 2
+        + [pltpu.SemaphoreType.DMA((PIECES,))] * 4,
+        compiler_params=pltpu.CompilerParams(collective_id=collective_id, has_side_effects=True),
+    )(terms.reshape(zero_count, rows, width))
+
+
+def shift_kernel(step, x_ref, out_ref):
+    x = x_ref[...]
+    rows, width = x.shape
+    shift = lax.axis_index("dp") * step
+    rolled = pltpu.roll(x, shift, axis=1)
+    above = pltpu.roll(rolled, 1, axis=0)
+    lane = lax.broadcasted_iota(jnp.int32, x.shape, 1)
+    out_ref[pl.ds(0, rows)] = jnp.where(lane >= shift, rolled, above).astype(out_ref.dtype)
+    if out_ref.shape[0] > rows:
+        out_ref[pl.ds(rows, out_ref.shape[0] - rows)] = jnp.zeros(
+            (out_ref.shape[0] - rows, width), out_ref.dtype
+        )
+
+
+def shift_piece(x, step, out_rows):
+    return pl.pallas_call(
+        lambda *refs: shift_kernel(step, *refs),
+        out_shape=jax.ShapeDtypeStruct((out_rows, x.shape[1]), jnp.bfloat16),
+        in_specs=[VM],
+        out_specs=VM,
+        name="shift_piece",
+    )(x)
+
+
+def dp_gather_kernel(
+    tail, x_ref, out_ref, gains_ref, own_sem, own_gain, z_send, z_recv, y_send, y_recv, g_send, g_recv
+):
+    me = lax.axis_index("dp")
+    count = out_ref.shape[0]
+    columns = count // 2
+    z_me, y_me = me // 2, me % 2
+    peer = z_me * 2 + 1 - y_me
+    spread = [lax.rem(z_me + k, columns) * 2 + y_me for k in range(1, columns)]
+    origin = [lax.rem(z_me + columns - k, columns) * 2 + y_me for k in range(1, columns)]
+    zero_me = lax.axis_index("zero")
+    zero_count = gains_ref.shape[0]
+    others = [lax.rem(zero_me + k, zero_count) for k in range(1, zero_count)]
+    greet([("dp", peer)] + [("dp", i) for i in spread] + [("zero", i) for i in others])
+    own = pltpu.make_async_copy(x_ref, out_ref.at[me], own_sem)
+    own.start()
+    first = remote(x_ref, out_ref.at[me], y_send.at[0], y_recv.at[0], "dp", peer)
+    first.start()
+    zs, ys = [], []
+    for k in range(columns - 1):
+        copy = remote(x_ref, out_ref.at[me], z_send.at[k], z_recv.at[k], "dp", spread[k])
+        copy.start()
+        zs.append(copy)
+    for k in (0, columns - 2) + tuple(range(1, columns - 2)):
+        zs[k].wait_recv()
+        piece = out_ref.at[origin[k]]
+        copy = remote(piece, piece, y_send.at[k + 1], y_recv.at[k + 1], "dp", peer)
+        copy.start()
+        ys.append(copy)
+    own.wait()
+    first.wait()
+    for copy in ys:
+        copy.wait()
+    last = out_ref.at[count - 1, pl.ds(tail, 16)]
+    own = pltpu.make_async_copy(last, gains_ref.at[zero_me], own_gain)
+    own.start()
+    gs = []
+    for k in range(zero_count - 1):
+        copy = remote(last, gains_ref.at[zero_me], g_send.at[k], g_recv.at[k], "zero", others[k])
+        copy.start()
+        gs.append(copy)
+    own.wait()
+    for copy in gs:
+        copy.wait()
+    for copy in zs:
+        copy.wait_send()
+
+
+def dp_gather(x, tail, collective_id):
+    count, zero_count = lax.axis_size("dp"), lax.axis_size("zero")
+    columns = count // 2
+    rows, width = x.shape
+    dma = pltpu.SemaphoreType.DMA
+    return pl.pallas_call(
+        lambda *refs: dp_gather_kernel(tail, *refs),
+        out_shape=(
+            jax.ShapeDtypeStruct((count, rows, width), x.dtype),
+            jax.ShapeDtypeStruct((zero_count, 16, width), x.dtype),
+        ),
+        in_specs=[VM],
+        out_specs=(VM, VM),
+        scratch_shapes=[
+            dma,
+            dma,
+            dma((columns - 1,)),
+            dma((columns - 1,)),
+            dma((columns,)),
+            dma((columns,)),
+            dma((zero_count - 1,)),
+            dma((zero_count - 1,)),
+        ],
+        compiler_params=pltpu.CompilerParams(collective_id=collective_id, has_side_effects=True),
+        name="dp_gather",
+    )(x)
+
+
+def dp_scatter_kernel(step, x_ref, out_ref, pair, total, far, y_send, y_recv, z_send, z_recv):
+    me = lax.axis_index("dp")
+    count, rows, width = x_ref.shape
+    columns = count // 2
+    z_me, y_me = me // 2, me % 2
+    peer = z_me * 2 + 1 - y_me
+    order = [lax.rem(z_me + k, columns) for k in (*range(1, columns), 0)]
+    greet([("dp", peer)] + [("dp", z * 2 + y_me) for z in order[:-1]])
+    ys, zs = [], []
+    for k in range(columns):
+        copy = remote(
+            x_ref.at[order[k] * 2 + 1 - y_me], pair.at[k], y_send.at[k], y_recv.at[k], "dp", peer
+        )
+        copy.start()
+        ys.append(copy)
+    for k in range(columns - 1):
+        ys[k].wait_recv()
+        total[k] = (
+            x_ref[order[k] * 2 + y_me].astype(jnp.float32) + pair[k].astype(jnp.float32)
+        ).astype(jnp.bfloat16)
+        copy = remote(
+            total.at[k], far.at[k], z_send.at[k], z_recv.at[k], "dp", order[k] * 2 + y_me
+        )
+        copy.start()
+        zs.append(copy)
+    ys[columns - 1].wait_recv()
+    acc = x_ref[me].astype(jnp.float32) + pair[columns - 1].astype(jnp.float32)
+    for k in range(columns - 1):
+        zs[k].wait_recv()
+        acc = acc + far[k].astype(jnp.float32)
+    if step:
+        shift = me * step
+        rolled = pltpu.roll(acc, lax.rem(width - shift, width), axis=1)
+        below = pltpu.roll(rolled, rows - 1, axis=0)
+        lane = lax.broadcasted_iota(jnp.int32, acc.shape, 1)
+        acc = jnp.where(lane + shift < width, rolled, below)
+    out_ref[...] = acc
+    for copy in ys:
+        copy.wait_send()
+    for copy in zs:
+        copy.wait_send()
+
+
+def dp_scatter(x, step, collective_id):
+    count, rows, width = x.shape
+    columns = count // 2
+    dma = pltpu.SemaphoreType.DMA
+    return pl.pallas_call(
+        lambda *refs: dp_scatter_kernel(step, *refs),
+        out_shape=jax.ShapeDtypeStruct((rows, width), jnp.float32),
+        in_specs=[VM],
+        out_specs=VM,
+        scratch_shapes=[
+            pltpu.VMEM((columns, rows, width), x.dtype),
+            pltpu.VMEM((columns - 1, rows, width), x.dtype),
+            pltpu.VMEM((columns - 1, rows, width), x.dtype),
+            dma((columns,)),
+            dma((columns,)),
+            dma((columns - 1,)),
+            dma((columns - 1,)),
+        ],
+        compiler_params=pltpu.CompilerParams(collective_id=collective_id, has_side_effects=True),
+        name="dp_scatter",
+    )(x)
+
+
 def per_device(tokens, cotangent, params, first_moment, second_moment):
     zero_count = lax.axis_size("zero")
     dp_count = lax.axis_size("dp")
@@ -103,20 +413,44 @@
     ff_part = FF // zero_count
     ffn_piece = 3 * D * FF // zero_count // dp_count
     attn_piece = shard_size - ffn_piece
-    own_bf = params.astype(jnp.bfloat16)
-    slice_all = lax.all_gather(own_bf, "dp", axis=1, tiled=True).reshape(dp_count, shard_size)
-    ffn_flat = slice_all[:, :ffn_piece].reshape(-1)
-    attn_flat = slice_all[:, ffn_piece:].reshape(-1)
+    attn_rows, attn_step = attn_piece // D, attn_piece % D
+    aligned = ffn_piece % D == 0 and attn_rows % 16 == 0 and dp_count == 8
+    lift_end = 2 * ff_part * D
     first_end = 3 * quarter * D
     second_end = first_end + D * quarter
-    w_qkv = attn_flat[:first_end].reshape(3 * quarter, D)
-    w_attn = attn_flat[first_end:second_end].reshape(D, quarter)
-    gains = lax.all_gather(attn_flat[second_end:].reshape(2, quarter), "zero", axis=1, tiled=True)
+    if aligned:
+        own = params.reshape(shard_size)
+        ffn_own = own[:ffn_piece].reshape(ffn_piece // D, D).astype(jnp.bfloat16)
+        pad_rows = attn_rows + 8
+        attn_own = jnp.pad(own[ffn_piece:], (0, pad_rows * D - attn_piece)).reshape(pad_rows, D)
+        attn_own = shift_piece(attn_own, attn_step, attn_rows + 16)
+        attn_all, gain_rows = dp_gather(attn_own, attn_rows, 1)
+        ffn_all = lax.all_gather(ffn_own, "dp", axis=0, tiled=True)
+        edge = jnp.concatenate([jnp.zeros((1, D), jnp.bfloat16), attn_all[:-1, attn_rows]])
+        body = attn_all[:, :attn_rows]
+        lead = lax.broadcasted_iota(jnp.int32, body.shape, 1) == 0
+        body = body + jnp.where(lead, edge[:, None, :], jnp.zeros((), jnp.bfloat16))
+        body = body.reshape(dp_count * attn_rows, D)
+        w_qkv = body[: 3 * quarter]
+        w_attn = body[3 * quarter :].reshape(D, quarter)
+        gains = gain_rows[:, 0, : 2 * quarter].reshape(zero_count, 2, quarter)
+        gains = jnp.transpose(gains, (1, 0, 2)).reshape(2, D)
+        w_input = ffn_all[: 2 * ff_part]
+        w_output = ffn_all[2 * ff_part :].reshape(D, ff_part)
+    else:
+        own_bf = params.astype(jnp.bfloat16)
+        slice_all = lax.all_gather(own_bf, "dp", axis=1, tiled=True).reshape(dp_count, shard_size)
+        ffn_flat = slice_all[:, :ffn_piece].reshape(-1)
+        attn_flat = slice_all[:, ffn_piece:].reshape(-1)
+        w_qkv = attn_flat[:first_end].reshape(3 * quarter, D)
+        w_attn = attn_flat[first_end:second_end].reshape(D, quarter)
+        gains = lax.all_gather(
+            attn_flat[second_end:].reshape(2, quarter), "zero", axis=1, tiled=True
+        )
+        w_input = ffn_flat[:lift_end].reshape(2 * ff_part, D)
+        w_output = ffn_flat[lift_end:].reshape(D, ff_part)
     gain_one32 = gains[0].astype(jnp.float32)
     gain_two32 = gains[1].astype(jnp.float32)
-    lift_end = 2 * ff_part * D
-    w_input = ffn_flat[:lift_end].reshape(2 * ff_part, D)
-    w_output = ffn_flat[lift_end:].reshape(D, ff_part)
     seq_count, own_len = (tokens.shape[0], tokens.shape[1])
     own_rows = seq_count * own_len
     length = own_len * zero_count
@@ -129,7 +463,7 @@
     inputs = tokens.astype(jnp.float32).reshape(own_rows, D)
     normed_one, inverse_one = norm_forward(inputs)
     normal_one = (normed_one * gain_one32).astype(jnp.bfloat16).reshape(seq_count, own_len, D)
-    full_one = lax.all_gather(normal_one, "zero", axis=1, tiled=True).reshape(row_count, D)
+    full_one = zero_gather(normal_one.reshape(own_rows, D), 2)
     projected = jnp.dot(full_one, w_qkv.T, preferred_element_type=jnp.float32)
     projected = projected.reshape(seq_count, length, 3, local_heads, HEAD)
     queries = (projected[:, :, 0] * cosine + rotate_half(projected[:, :, 0]) * sine_table).astype(
@@ -157,27 +491,17 @@
     ).astype(jnp.bfloat16)
     context_rows = context.reshape(row_count, quarter)
     attn_terms = jnp.dot(context_rows, w_attn.T, preferred_element_type=jnp.float32)
-    attn_sum = lax.psum_scatter(
-        attn_terms.reshape(seq_count, length, D).astype(jnp.bfloat16),
-        "zero",
-        scatter_dimension=1,
-        tiled=True,
-    ).astype(jnp.float32)
+    attn_sum = zero_scatter(attn_terms.astype(jnp.bfloat16), 6)
     hidden = inputs + attn_sum.reshape(own_rows, D)
     normed_two, inverse_two = norm_forward(hidden)
     normal_two = (normed_two * gain_two32).astype(jnp.bfloat16).reshape(seq_count, own_len, D)
-    full_two = lax.all_gather(normal_two, "zero", axis=1, tiled=True).reshape(row_count, D)
+    full_two = zero_gather(normal_two.reshape(own_rows, D), 3)
     lifted = jnp.dot(full_two, w_input.T, preferred_element_type=jnp.float32)
     gate_act, gate_slope = gelu_parts(lifted[:, :ff_part])
     up_half = lifted[:, ff_part:]
     mixed = (gate_act * up_half).astype(jnp.bfloat16)
     ffn_terms = jnp.dot(mixed, w_output.T, preferred_element_type=jnp.float32)
-    ffn_sum = lax.psum_scatter(
-        ffn_terms.reshape(seq_count, length, D).astype(jnp.bfloat16),
-        "zero",
-        scatter_dimension=1,
-        tiled=True,
-    ).astype(jnp.float32)
+    ffn_sum = zero_scatter(ffn_terms.astype(jnp.bfloat16), 7)
     output = hidden + ffn_sum.reshape(own_rows, D)
     grad_scale = float(dp_count * row_count) ** (-0.5)
     cot_full = lax.all_gather(cotangent, "zero", axis=1, tiled=True).reshape(row_count, D)
@@ -187,25 +511,22 @@
         [grad_mixed * up_half * gate_slope, grad_mixed * gate_act], axis=-1
     ).astype(jnp.bfloat16)
     grad_input_w = jnp.dot(grad_lifted.T, full_two, preferred_element_type=jnp.float32)
-    ffn_vec = jnp.concatenate([grad_input_w.ravel(), grad_output_w.ravel()]) * grad_scale
-    ffn_vec = ffn_vec.reshape(dp_count, ffn_piece)
+    if aligned:
+        ffn_grads = jnp.concatenate([grad_input_w, grad_output_w.reshape(ff_part, D)]) * grad_scale
+        ffn_shard = lax.psum_scatter(
+            ffn_grads.astype(jnp.bfloat16), "dp", scatter_dimension=0, tiled=True
+        ).astype(jnp.float32)
+    else:
+        ffn_vec = jnp.concatenate([grad_input_w.ravel(), grad_output_w.ravel()]) * grad_scale
+        ffn_vec = ffn_vec.reshape(dp_count, ffn_piece)
     norm_two_terms = jnp.dot(grad_lifted, w_input, preferred_element_type=jnp.float32)
-    grad_norm_two = (
-        lax.psum_scatter(
-            norm_two_terms.reshape(seq_count, length, D).astype(jnp.bfloat16),
-            "zero",
-            scatter_dimension=1,
-            tiled=True,
-        )
-        .astype(jnp.float32)
-        .reshape(own_rows, D)
-    )
+    grad_norm_two = zero_scatter(norm_two_terms.astype(jnp.bfloat16), 8)
     gain_two_term = jnp.sum(grad_norm_two * normed_two, axis=0)
     grad_hidden = cotangent.reshape(own_rows, D).astype(jnp.float32) + norm_backward(
         grad_norm_two, gain_two32, normed_two, inverse_two
     )
     grad_hidden_b = grad_hidden.astype(jnp.bfloat16).reshape(seq_count, own_len, D)
-    hidden_full = lax.all_gather(grad_hidden_b, "zero", axis=1, tiled=True).reshape(row_count, D)
+    hidden_full = zero_gather(grad_hidden_b.reshape(own_rows, D), 5)
     grad_attn_w = jnp.dot(hidden_full.T, context_rows, preferred_element_type=jnp.float32)
     grad_context = jnp.dot(hidden_full, w_attn, preferred_element_type=jnp.float32).astype(
         jnp.bfloat16
@@ -247,28 +568,36 @@
     )
     grad_qkv_w = jnp.dot(grad_packed.T, full_one, preferred_element_type=jnp.float32)
     norm_one_terms = jnp.dot(grad_packed, w_qkv, preferred_element_type=jnp.float32)
-    grad_norm_one = (
-        lax.psum_scatter(
-            norm_one_terms.reshape(seq_count, length, D).astype(jnp.bfloat16),
-            "zero",
-            scatter_dimension=1,
-            tiled=True,
-        )
-        .astype(jnp.float32)
-        .reshape(own_rows, D)
-    )
+    grad_norm_one = zero_scatter(norm_one_terms.astype(jnp.bfloat16), 9)
     gain_one_term = jnp.sum(grad_norm_one * normed_one, axis=0)
     grad_inputs = grad_hidden + norm_backward(grad_norm_one, gain_one32, normed_one, inverse_one)
     gain_grads = lax.psum_scatter(
         jnp.stack([gain_one_term, gain_two_term]), "zero", scatter_dimension=1, tiled=True
     )
-    attn_vec = (
-        jnp.concatenate([grad_qkv_w.ravel(), grad_attn_w.ravel(), gain_grads.ravel()]) * grad_scale
-    )
-    attn_vec = attn_vec.reshape(dp_count, attn_piece)
-    grad_shard = lax.psum_scatter(
-        jnp.concatenate([ffn_vec, attn_vec], axis=1), "dp", scatter_dimension=0, tiled=True
-    )
+    if aligned:
+        gain_row = jnp.pad(gain_grads.reshape(1, 2 * quarter), ((0, 0), (0, D - 2 * quarter)))
+        grad_rows = jnp.concatenate([grad_qkv_w, grad_attn_w.reshape(quarter, D), gain_row])
+        grad_rows = (grad_rows * grad_scale).astype(jnp.bfloat16)
+        chunks = grad_rows[:-1].reshape(dp_count, attn_rows, D)
+        chunks = jnp.concatenate(
+            [
+                chunks,
+                jnp.concatenate([chunks[1:, :1], grad_rows[-1:][None]]),
+                jnp.zeros((dp_count, 15, D), jnp.bfloat16),
+            ],
+            axis=1,
+        )
+        attn_shard = dp_scatter(chunks, attn_step, 10).reshape(-1)[:attn_piece]
+        grad_shard = jnp.concatenate([ffn_shard.reshape(-1), attn_shard])
+    else:
+        attn_vec = (
+            jnp.concatenate([grad_qkv_w.ravel(), grad_attn_w.ravel(), gain_grads.ravel()])
+            * grad_scale
+        )
+        attn_vec = attn_vec.reshape(dp_count, attn_piece)
+        grad_shard = lax.psum_scatter(
+            jnp.concatenate([ffn_vec, attn_vec], axis=1), "dp", scatter_dimension=0, tiled=True
+        )
     grad_shard = grad_shard.reshape(params.shape)
     new_first = beta_one * first_moment + (1.0 - beta_one) * grad_shard
     new_second = beta_two * second_moment + (1.0 - beta_two) * grad_shard * grad_shard

time: 491 us -> 293 us (0.60)
  waiting for transfers between devices: 325 us -> 0.06 us
  Pallas kernels: 0 us -> 129 us
  local copies, waits for them, and re-layouts: 52.7 us -> 38.4 us
  blocking collectives: 39.4 us -> 48.7 us
    unnamed x9 -> x4, waiting for transfers between devices: 191 us -> 0.06 us
    pallas_call x0 -> x10, Pallas kernels: none -> 129 us  [the longest x4 41.2 us: zero_scatter(): pl.pallas_call(zero_scatter_kernel, out_shape=jax.ShapeDtypeStruct((rows,...]
    all_gather x1, waiting for transfers between devices: 84.5 us -> 0.01 us  [per_device(): ffn_all = lax.all_gather(ffn_own, 'dp', axis=0, tiled=True)]
    reduce_scatter x4 -> x0, waiting for transfers between devices: 48.9 us -> none  [the longest x1 21.9 us: per_device(): lax.psum_scatter(norm_one_terms.reshape(seq_count, length, D).astype(jnp....]
    unnamed x0 -> x1, blocking collectives: none -> 39.9 us
    all_gather x4 -> x0, blocking collectives: 30 us -> none  [the longest x1 8.68 us: per_device(): lax.all_gather(normal_one, 'zero', axis=1, tiled=True).reshape(row_count, D)]
    unnamed x122 -> x125, local copies, waits for them, and re-layouts: 20.3 us -> 9.89 us
    mul x2 -> x0, local copies, waits for them, and re-layouts: 6.38 us -> none  [the longest x1 4.49 us: per_device(): jnp.concatenate([grad_qkv_w.ravel(), grad_attn_w.ravel(), gain_grads.rave...]
  transfers between devices with their start and end apart: 7 -> 3, of which waited for: 7 -> 0; matrix products, arithmetic and copies ran while one was open for 10% -> 28% of each run, Pallas kernels for 0% -> 30%
where the time goes in v1:
time: 293 us; the launch traced here: 292 us
  Pallas kernels  129 us (44%)
  blocking collectives  48.7 us (17%)
  local copies, waits for them, and re-layouts  38.4 us (13%)
  other arithmetic  31.9 us (11%)
  matrix products  25.1 us (9%)
  between operations  15.9 us (5%)
  starting transfers between devices  3.11 us (1%)
    pallas_call x4, Pallas kernels, zero_scatter(): pl.pallas_call(zero_scatter_kernel, out_shape=jax.ShapeDtypeStruct((rows,...  41.2 us
    unnamed x1, blocking collectives  39.9 us
    pallas_call x1, Pallas kernels, dp_gather(): pl.pallas_call(lambda *refs: dp_gather_kernel(tail, *refs), out_shape=(ja...  34.2 us
    pallas_call x3, Pallas kernels, zero_gather(): pl.pallas_call(zero_gather_kernel, out_shape=jax.ShapeDtypeStruct((zero_c...  29.6 us
    pallas_call x1, Pallas kernels, dp_scatter(): pl.pallas_call(lambda *refs: dp_scatter_kernel(step, *refs), out_shape=ja...  21.8 us
    unnamed x125, local copies, waits for them, and re-layouts  9.89 us
    all_gather x1, blocking collectives, per_device(): lax.all_gather(cotangent, 'zero', axis=1, tiled=True).reshape(row_count, D)  8.86 us
  transfers between devices with their start and end apart: 3, of which 0 were waited for; matrix products, arithmetic and copies ran while one was open for 28% of the time, Pallas kernels for 30%

profile of v1, /device:TPU:0, one launch (start us, length us, event | category | flops | bytes accessed | tf_op | source)
XLA Modules:
  0.0 291.9 jit_solution(12897026417759635197)
XLA Ops:
  7.2 1.8 fusion.50
  10.0 1.7 slice_reduce_fusion
  12.5 1.8 shift_piece.1.refs_0_
  14.3 34.2 %dp_gather.1 = (bf16[8,112,768]{2,1,0:T(8,128)(2,1)}, bf16[4,16,768]{2,1,0:T(8,128)(2,1)}) custom-call(bf16[112,768]{1,0:T(8,128)(2,1)} %shift_piece.1.refs_0_), custom_call_target="tpu_custom_call" | custom-call | tf_op jit(solution)/shard_map/dp_gather/pallas_call | solution.py:319
  54.7 9.8 %shard_map.100 = bf16[4,128,768]{2,1,0:T(8,128)(2,1)} custom-call(bf16[128,768]{1,0:T(8,128)(2,1)} %fusion.34.x_ref), custom_call_target="tpu_custom_call" | custom-call | tf_op jit(solution)/shard_map/pallas_call | solution.py:169
  64.5 2.1 convolution_bitcast_fusion
  78.3 10.4 %shard_map.101 = f32[128,768]{1,0:T(8,128)} custom-call(bf16[4,128,768]{2,1,0:T(8,128)(2,1)} %bitcast.210), custom_call_target="tpu_custom_call" | custom-call | tf_op jit(solution)/shard_map/pallas_call | solution.py:230
  90.2 8.9 %all_gather.7 = bf16[1,512,768]{2,1,0:T(8,128)(2,1)} all-gather(bf16[1,128,768]{2,1,0:T(8,128)(2,1)S(1)} %copy-done.37), channel_id=1, replica_groups=mesh['dp'=8,'zero'=4] {'zero'}, dimensions={1}, use_global_device_ids=true | all-gather | bytes 983040 | tf_op jit(solution)/shard_map/all_gather | solution.py:507
  99.9 10.0 %shard_map.102 = bf16[4,128,768]{2,1,0:T(8,128)(2,1)} custom-call(bf16[128,768]{1,0:T(8,128)(2,1)} %multiply_convert_fusion.3.x_ref), custom_call_target="tpu_custom_call" | custom-call | tf_op jit(solution)/shard_map/pallas_call | solution.py:169
  113.0 2.4 reshape.705
  115.4 2.9 fusion.10
  118.3 1.7 reshape.680
  120.0 3.1 %fusion.20 = (bf16[512,288]{0,1:T(8,128)(2,1)S(1)}, bf16[512,288]{0,1:T(8,128)(2,1)S(1)}, bf16[512,288]{0,1:T(8,128)(2,1)}) fusion(f32[512,576]{0,1:T(8,128)} %fusion.10, bf16[768,288]{1,0:T(8,128)(2,1)} %reshape.680, bf16[1,512,768]{2,1,0:T(8,128)(2,1)} %all_gather.7), kind=kOutput, calls=%fused_computation.47 | convolution fusion | flops 228851712 | bytes 3293184 | tf_op jit(solution)/shard_map/dot_general | solution.py:509
  123.1 1.7 convolution_convert_fusion.1
  124.9 10.4 %shard_map.104 = f32[128,768]{1,0:T(8,128)} custom-call(bf16[4,128,768]{2,1,0:T(8,128)(2,1)} %bitcast.216), custom_call_target="tpu_custom_call" | custom-call | tf_op jit(solution)/shard_map/pallas_call | solution.py:230
  135.3 1.8 multiply_reduce_fusion
  138.2 2.7 convolution_convert_fusion.3
  140.9 9.9 %shard_map.103 = f32[128,768]{1,0:T(8,128)} custom-call(bf16[4,128,768]{2,1,0:T(8,128)(2,1)} %bitcast.209), custom_call_target="tpu_custom_call" | custom-call | tf_op jit(solution)/shard_map/pallas_call | solution.py:230
  150.8 2.1 fusion.78
  152.9 9.8 %shard_map.105 = bf16[4,128,768]{2,1,0:T(8,128)(2,1)} custom-call(bf16[128,768]{1,0:T(8,128)(2,1)} %get-tuple-element.21.x_ref), custom_call_target="tpu_custom_call" | custom-call | tf_op jit(solution)/shard_map/pallas_call | solution.py:169
  177.9 1.7 convolution_convert_fusion
  179.7 10.4 %shard_map.106 = f32[128,768]{1,0:T(8,128)} custom-call(bf16[4,128,768]{2,1,0:T(8,128)(2,1)} %bitcast.217), custom_call_target="tpu_custom_call" | custom-call | tf_op jit(solution)/shard_map/pallas_call | solution.py:230
  192.9 1.9 fusion.87
  194.8 2.6 copy.58
  197.4 3.0 %reshape.693 = f32[288,768]{1,0:T(8,128)} reshape(f32[768,288]{1,0:T(8,128)} %copy.58) | data formatting | bytes 1769472 | tf_op jit(solution)/shard_map/reshape | solution.py:515
  200.4 2.5 fusion.1
  202.9 39.9 %fusion = bf16[112,768]{1,0:T(8,128)(2,1)S(1)} fusion(bf16[864,768]{1,0:T(8,128)(2,1)} %fusion.1), kind=kCustom, calls=%all-reduce-scatter | all-reduce-scatter fusion | flops 688129 | bytes 1499648
  242.8 3.0 %collective-permute-start = (bf16[28,768]{1,0:T(8,128)(2,1)S(1)}, bf16[28,768]{1,0:T(8,128)(2,1)S(1)}, u32[]{:S(2)}, u32[]{:S(2)}) collective-permute-start(bf16[28,768]{1,0:T(8,128)(2,1)S(1)} %slice.203), channel_id=1, source_target_pairs={{0,4},{4,8},{8,12},{12,16},{16,20},{20,24},{24,28},{1,5},{5,9},{9,... | collective-permute-start | bytes 129032
  245.8 1.9 fusion.39
  251.5 21.8 %dp_scatter.1 = f32[112,768]{1,0:T(8,128)} custom-call(bf16[8,112,768]{2,1,0:T(8,128)(2,1)} %maximum_maximum_fusion.refs_0_), custom_call_target="tpu_custom_call" | custom-call | tf_op jit(solution)/shard_map/dp_scatter/pallas_call | solution.py:389
  275.5 3.7 %reshape.699 = f32[1,1,156720]{2,1,0:T(1,128)} reshape(f32[156720]{0:T(1024)S(1)} %pad_maximum_fusion) | data formatting | bytes 1253760 | tf_op jit(solution)/shard_map/reshape | solution.py:601
  279.5 5.6 %multiply_subtract_fusion = (f32[1,1,156720]{2,1,0:T(1,128)}, f32[1,1,156720]{2,1,0:T(1,128)}, f32[1,1,156720]{2,1,0:T(1,128)}) fusion(f32[1,1,156720]{2,1,0:T(1,128)S(1)} %copy-done.14, f32[156720]{0:T(1024)S(1)} %copy-done.13, f32[156720]{0:T(1024)S(1)} %copy-done.12, f32[1,1,156720]{2,1,0:T(1,128)S(1)} %reshape_dynamic-update-slice_fusion, ...), kind=kLoop, calls=%fused_computation.40 | loop fusion | flops 2350800 | bytes 5641920 | tf_op jit(solution)/shard_map/sub | solution.py:615
  (238 shorter events, 48.7 us)
Async XLA Ops:
  7.2 105.8 %all-gather.3.cloned.1.call-start = ((), (), s32[]{:S(2)}) async-start(), calls=%async_computation.1 | async-start | bytes 1548288 | tf_op jit(solution)/shard_map/all_gather | solution.py:428
  9.9 238.2 %reduce-scatter.6.cloned.1.call-start = ((), (), s32[]{:S(2)}) async-start(), calls=%async_computation.2 | async-start | bytes 491520
  50.9 3.7 %copy-start.5 = (bf16[8,96,768]{2,1,0:T(8,128)(2,1)}, bf16[8,96,768]{2,1,0:T(8,128)(2,1)S(1)}, u32[]{:S(2)}) copy-start(bf16[8,96,768]{2,1,0:T(8,128)(2,1)S(1)} %select_add_fusion) | copy-start | bytes 3538948
  53.6 12.9 %copy-start.47 = (f32[128]{0:T(128)}, f32[128]{0:T(128)S(1)}, u32[]{:S(2)}) copy-start(f32[128]{0:T(128)S(1)} %broadcast_multiply_fusion.5) | copy-start | bytes 1540
  53.8 12.7 %copy-start.50 = (f32[128]{0:T(128)}, f32[128]{0:T(128)S(1)}, u32[]{:S(2)}) copy-start(f32[128]{0:T(128)S(1)} %add_rsqrt_fusion.1) | copy-start | bytes 1540
  67.9 9.0 %copy-start.9 = (bf16[768,192]{1,0:T(8,128)(2,1)}, bf16[768,192]{1,0:T(8,128)(2,1)S(1)}, u32[]{:S(2)}) copy-start(bf16[768,192]{1,0:T(8,128)(2,1)S(1)} %reshape.677) | copy-start | bytes 884740
  76.8 13.1 %copy-start.17 = (bf16[1,4,128,3,64]{2,4,3,1,0:T(8,128)(2,1)}, bf16[1,4,128,3,64]{2,4,3,1,0:T(8,128)(2,1)S(1)}, u32[]{:S(2)}) copy-start(bf16[1,4,128,3,64]{2,4,3,1,0:T(8,128)(2,1)S(1)} %fusion.5) | copy-start | bytes 589828
  76.9 12.9 %copy-start.19 = (bf16[1,4,128,3,64]{2,1,4,3,0:T(4,128)(2,1)}, bf16[1,4,128,3,64]{2,1,4,3,0:T(4,128)(2,1)S(1)}, u32[]{:S(2)}) copy-start(bf16[1,4,128,3,64]{2,1,4,3,0:T(4,128)(2,1)S(1)} %copy.50) | copy-start | bytes 589828
  77.0 12.9 %copy-start.46 = (f32[4,192]{1,0:T(4,128)S(1)}, f32[4,192]{1,0:T(4,128)}, u32[]{:S(2)}) copy-start(f32[4,192]{1,0:T(4,128)} %get-tuple-element.16) | copy-start | bytes 9220
  78.3 11.9 %copy-start.37 = (bf16[1,128,768]{2,1,0:T(8,128)(2,1)S(1)}, bf16[1,128,768]{2,1,0:T(8,128)(2,1)}, u32[]{:S(2)}) copy-start(bf16[1,128,768]{2,1,0:T(8,128)(2,1)} %param.6) | copy-start | bytes 589828
  89.9 20.7 %copy-start.54 = (u32[32]{0:T(128)S(1)}, u32[32]{0:T(128)}, u32[]{:S(2)}) copy-start(u32[32]{0:T(128)} %constant.118) | copy-start | bytes 388
  90.0 45.3 %copy-start.49 = (f32[128]{0:T(128)}, f32[128]{0:T(128)S(1)}, u32[]{:S(2)}) copy-start(f32[128]{0:T(128)S(1)} %broadcast_multiply_fusion.4) | copy-start | bytes 1540
  90.2 45.1 %copy-start.52 = (f32[128]{0:T(128)}, f32[128]{0:T(128)S(1)}, u32[]{:S(2)}) copy-start(f32[128]{0:T(128)S(1)} %add_rsqrt_fusion) | copy-start | bytes 1540
  115.4 2.9 slice-start
  120.0 3.1 %copy-start.4 = (bf16[864,768]{1,0:T(8,128)(2,1)S(1)}, bf16[864,768]{1,0:T(8,128)(2,1)}, u32[]{:S(2)}) copy-start(bf16[864,768]{1,0:T(8,128)(2,1)} %reshape.705) | copy-start | bytes 3981316
  137.1 13.7 %copy-start.7 = (f32[128,768]{1,0:T(8,128)S(1)}, f32[128,768]{1,0:T(8,128)}, u32[]{:S(2)}) copy-start(f32[128,768]{1,0:T(8,128)} %shard_map.104) | copy-start | bytes 1179652
  137.1 13.7 %copy-start.38 = (bf16[1,128,768]{2,1,0:T(8,128)(2,1)S(1)}, bf16[1,128,768]{2,1,0:T(8,128)(2,1)}, u32[]{:S(2)}) copy-start(bf16[1,128,768]{2,1,0:T(8,128)(2,1)} %param.6) | copy-start | bytes 589828
  175.1 2.7 copy-start.36
  175.1 2.8 copy-start.6
  177.9 12.2 %copy-start.48 = (f32[128]{0:T(128)S(1)}, f32[128]{0:T(128)}, u32[]{:S(2)}) copy-start(f32[128]{0:T(128)} %copy-done.47) | copy-start | bytes 1540
  177.9 12.2 %copy-start.51 = (f32[128]{0:T(128)S(1)}, f32[128]{0:T(128)}, u32[]{:S(2)}) copy-start(f32[128]{0:T(128)} %copy-done.50) | copy-start | bytes 1540
  179.7 12.2 %copy-start.45 = (f32[768]{0:T(1024)S(1)}, f32[768]{0:T(1024)}, u32[]{:S(2)}) copy-start(f32[768]{0:T(1024)} %get-tuple-element.10) | copy-start | bytes 9220
  202.9 43.0 %copy-start.3 = (bf16[1,128,768]{2,1,0:T(8,128)(2,1)S(1)}, bf16[1,128,768]{2,1,0:T(8,128)(2,1)}, u32[]{:S(2)}) copy-start(bf16[1,128,768]{2,1,0:T(8,128)(2,1)} %param.5) | copy-start | bytes 589828
  202.9 43.0 %copy-start.8 = (f32[128,768]{1,0:T(8,128)S(1)}, f32[128,768]{1,0:T(8,128)}, u32[]{:S(2)}) copy-start(f32[128,768]{1,0:T(8,128)} %shard_map.106) | copy-start | bytes 1179652
  202.9 43.0 %copy-start.53 = (f32[128]{0:T(128)S(1)}, f32[128]{0:T(128)}, u32[]{:S(2)}) copy-start(f32[128]{0:T(128)} %broadcast_multiply_fusion.1) | copy-start | bytes 1540
  202.9 44.9 %copy-start.10 = (f32[768,192]{1,0:T(8,128)S(1)}, f32[768,192]{1,0:T(8,128)}, u32[]{:S(2)}) copy-start(f32[768,192]{1,0:T(8,128)} %fusion.59) | copy-start | bytes 1769476
  242.8 31.6 %collective-permute-start = (bf16[28,768]{1,0:T(8,128)(2,1)S(1)}, bf16[28,768]{1,0:T(8,128)(2,1)S(1)}, u32[]{:S(2)}, u32[]{:S(2)}) collective-permute-start(bf16[28,768]{1,0:T(8,128)(2,1)S(1)} %slice.203), channel_id=1, source_target_pairs={{0,4},{4,8},{8,12},{12,16},{16,20},{20,24},{24,28},{1,5},{5,9},{9,... | collective-permute-start | bytes 129032
  275.4 4.0 %copy-start.40 = (f32[1,1,156720]{2,1,0:T(1,128)S(1)}, f32[1,1,156720]{2,1,0:T(1,128)}, u32[]{:S(2)}) copy-start(f32[1,1,156720]{2,1,0:T(1,128)} %param.9) | copy-start | bytes 1880644
  275.4 4.0 %copy-start.12 = (f32[156720]{0:T(1024)S(1)}, f32[156720]{0:T(1024)}, u32[]{:S(2)}) copy-start(f32[156720]{0:T(1024)} %get-tuple-element.50) | copy-start | bytes 1880644
  275.4 4.0 %copy-start.13 = (f32[156720]{0:T(1024)S(1)}, f32[156720]{0:T(1024)}, u32[]{:S(2)}) copy-start(f32[156720]{0:T(1024)} %get-tuple-element.51) | copy-start | bytes 1880644
  275.5 4.0 %copy-start.14 = (f32[1,1,156720]{2,1,0:T(1,128)S(1)}, f32[1,1,156720]{2,1,0:T(1,128)}, u32[]{:S(2)}) copy-start(f32[1,1,156720]{2,1,0:T(1,128)} %param.7) | copy-start | bytes 1880644
  275.5 4.0 %copy-start.39 = (f32[1,1,156720]{2,1,0:T(1,128)S(1)}, f32[1,1,156720]{2,1,0:T(1,128)}, u32[]{:S(2)}) copy-start(f32[1,1,156720]{2,1,0:T(1,128)} %param.8) | copy-start | bytes 1880644
  (29 other events, 39.4 us)
Sparse Core Ops, SparseCore 0:
  10.7 53.4 all-gather.2
  193.0 27.2 reduce-scatter.5

commit v2 on v1

--- a/solution.py
+++ b/solution.py
@@ -178,12 +178,12 @@
 
 
 def zero_scatter_kernel(
-    terms_ref, out_ref, mine, mixed, total, far, mate_send, mate_recv, mix_send, mix_recv, far_send, far_recv
+    terms_ref, out_ref, mine, mixed, total, far, mate_send, mate_recv, mix_send, mix_recv, far_send, far_recv, extra=False
 ):
     me, mate, across, diagonal = zero_places()
     rows = terms_ref.shape[1]
     part = rows // PIECES
-    greet([("zero", mate), ("zero", across)])
+    greet([("zero", mate), ("zero", across)] + [("zero", diagonal)] * extra)
     mixes, fars = [], []
     for k in range(PIECES):
         copy = remote(
@@ -239,6 +239,65 @@
     )(terms.reshape(zero_count, rows, width))
 
 
+def zero_scatter_gain_kernel(
+    terms_ref,
+    normed_ref,
+    other_ref,
+    out_ref,
+    gain_ref,
+    mine,
+    mixed,
+    total,
+    far,
+    gain_own,
+    gain_in,
+    mate_send,
+    mate_recv,
+    gain_send,
+    gain_recv,
+    *sems,
+):
+    me, mate, across, diagonal = zero_places()
+    zero_scatter_kernel(
+        terms_ref, out_ref, mine, mixed, total, far, mate_send, mate_recv, *sems, extra=True
+    )
+    gain_own[...] = jnp.zeros_like(gain_own)
+    gain_own[pl.ds(0, 1)] = jnp.sum(out_ref[...] * normed_ref[...], axis=0, keepdims=True)
+    gain_own[pl.ds(1, 1)] = other_ref[...]
+    copies = []
+    for k, index in enumerate((mate, across, diagonal)):
+        copy = remote(gain_own, gain_in.at[k], gain_send.at[k], gain_recv.at[k], "zero", index)
+        copy.start()
+        copies.append(copy)
+    total_gain = gain_own[...]
+    for k, copy in enumerate(copies):
+        copy.wait()
+        total_gain = total_gain + gain_in[k]
+    gain_ref[...] = total_gain
+
+
+def zero_scatter_gain(terms, normed, other, collective_id):
+    zero_count = lax.axis_size("zero")
+    rows, width = terms.shape[0] // zero_count, terms.shape[1]
+    buf = pltpu.VMEM((rows, width), jnp.bfloat16)
+    dma = pltpu.SemaphoreType.DMA
+    return pl.pallas_call(
+        zero_scatter_gain_kernel,
+        out_shape=(
+            jax.ShapeDtypeStruct((rows, width), jnp.float32),
+            jax.ShapeDtypeStruct((8, width), jnp.float32),
+        ),
+        in_specs=[VM] * 3,
+        out_specs=(VM, VM),
+        scratch_shapes=[buf] * 4
+        + [pltpu.VMEM((8, width), jnp.float32), pltpu.VMEM((3, 8, width), jnp.float32)]
+        + [dma] * 2
+        + [dma((3,))] * 2
+        + [dma((PIECES,))] * 4,
+        compiler_params=pltpu.CompilerParams(collective_id=collective_id, has_side_effects=True),
+    )(terms.reshape(zero_count, rows, width), normed, other)
+
+
 def shift_kernel(step, x_ref, out_ref):
     x = x_ref[...]
     rows, width = x.shape
@@ -264,7 +323,23 @@
 
 
 def dp_gather_kernel(
-    tail, x_ref, out_ref, gains_ref, own_sem, own_gain, z_send, z_recv, y_send, y_recv, g_send, g_recv
+    tail,
+    x_ref,
+    cot_ref,
+    out_ref,
+    gains_ref,
+    cots_ref,
+    own_sem,
+    own_gain,
+    own_cot,
+    z_send,
+    z_recv,
+    y_send,
+    y_recv,
+    g_send,
+    g_recv,
+    c_send,
+    c_recv,
 ):
     me = lax.axis_index("dp")
     count = out_ref.shape[0]
@@ -286,6 +361,13 @@
         copy = remote(x_ref, out_ref.at[me], z_send.at[k], z_recv.at[k], "dp", spread[k])
         copy.start()
         zs.append(copy)
+    own_c = pltpu.make_async_copy(cot_ref, cots_ref.at[zero_me], own_cot)
+    own_c.start()
+    cs = []
+    for k in range(zero_count - 1):
+        copy = remote(cot_ref, cots_ref.at[zero_me], c_send.at[k], c_recv.at[k], "zero", others[k])
+        copy.start()
+        cs.append(copy)
     for k in (0, columns - 2) + tuple(range(1, columns - 2)):
         zs[k].wait_recv()
         piece = out_ref.at[origin[k]]
@@ -307,11 +389,14 @@
     own.wait()
     for copy in gs:
         copy.wait()
+    own_c.wait()
+    for copy in cs:
+        copy.wait()
     for copy in zs:
         copy.wait_send()
 
 
-def dp_gather(x, tail, collective_id):
+def dp_gather(x, cot, tail, collective_id):
     count, zero_count = lax.axis_size("dp"), lax.axis_size("zero")
     columns = count // 2
     rows, width = x.shape
@@ -321,22 +406,23 @@
         out_shape=(
             jax.ShapeDtypeStruct((count, rows, width), x.dtype),
             jax.ShapeDtypeStruct((zero_count, 16, width), x.dtype),
+            jax.ShapeDtypeStruct((zero_count, *cot.shape), cot.dtype),
         ),
-        in_specs=[VM],
-        out_specs=(VM, VM),
+        in_specs=[VM, VM],
+        out_specs=(VM, VM, VM),
         scratch_shapes=[
+            dma,
             dma,
             dma,
             dma((columns - 1,)),
             dma((columns - 1,)),
             dma((columns,)),
             dma((columns,)),
-            dma((zero_count - 1,)),
-            dma((zero_count - 1,)),
+            *[dma((zero_count - 1,))] * 4,
         ],
         compiler_params=pltpu.CompilerParams(collective_id=collective_id, has_side_effects=True),
         name="dp_gather",
-    )(x)
+    )(x, cot)
 
 
 def dp_scatter_kernel(step, x_ref, out_ref, pair, total, far, y_send, y_recv, z_send, z_recv):
@@ -424,7 +510,10 @@
         pad_rows = attn_rows + 8
         attn_own = jnp.pad(own[ffn_piece:], (0, pad_rows * D - attn_piece)).reshape(pad_rows, D)
         attn_own = shift_piece(attn_own, attn_step, attn_rows + 16)
-        attn_all, gain_rows = dp_gather(attn_own, attn_rows, 1)
+        attn_all, gain_rows, cot_full = dp_gather(
+            attn_own, cotangent.reshape(-1, D), attn_rows, 1
+        )
+        ffn_own, attn_all = lax.optimization_barrier((ffn_own, attn_all))
         ffn_all = lax.all_gather(ffn_own, "dp", axis=0, tiled=True)
         edge = jnp.concatenate([jnp.zeros((1, D), jnp.bfloat16), attn_all[:-1, attn_rows]])
         body = attn_all[:, :attn_rows]
@@ -501,10 +590,13 @@
     up_half = lifted[:, ff_part:]
     mixed = (gate_act * up_half).astype(jnp.bfloat16)
     ffn_terms = jnp.dot(mixed, w_output.T, preferred_element_type=jnp.float32)
-    ffn_sum = zero_scatter(ffn_terms.astype(jnp.bfloat16), 7)
-    output = hidden + ffn_sum.reshape(own_rows, D)
+    ffn_sum = lax.psum_scatter(
+        ffn_terms.astype(jnp.bfloat16), "zero", scatter_dimension=0, tiled=True
+    )
     grad_scale = float(dp_count * row_count) ** (-0.5)
-    cot_full = lax.all_gather(cotangent, "zero", axis=1, tiled=True).reshape(row_count, D)
+    if not aligned:
+        cot_full = lax.all_gather(cotangent, "zero", axis=1, tiled=True)
+    cot_full = cot_full.reshape(row_count, D)
     grad_output_w = jnp.dot(cot_full.T, mixed, preferred_element_type=jnp.float32)
     grad_mixed = jnp.dot(cot_full, w_output, preferred_element_type=jnp.float32)
     grad_lifted = jnp.concatenate(
@@ -513,9 +605,17 @@
     grad_input_w = jnp.dot(grad_lifted.T, full_two, preferred_element_type=jnp.float32)
     if aligned:
         ffn_grads = jnp.concatenate([grad_input_w, grad_output_w.reshape(ff_part, D)]) * grad_scale
+        ffn_rows = ffn_piece // D
+        ffn_pad = -ffn_rows % 16
+        ffn_grads = ffn_grads.astype(jnp.bfloat16).reshape(dp_count, ffn_rows, D)
+        ffn_grads = jnp.pad(ffn_grads, ((0, 0), (0, ffn_pad), (0, 0)))
+        ffn_grads, grad_lifted = lax.optimization_barrier((ffn_grads, grad_lifted))
         ffn_shard = lax.psum_scatter(
-            ffn_grads.astype(jnp.bfloat16), "dp", scatter_dimension=0, tiled=True
-        ).astype(jnp.float32)
+            ffn_grads.reshape(dp_count * (ffn_rows + ffn_pad), D),
+            "dp",
+            scatter_dimension=0,
+            tiled=True,
+        )[:ffn_rows].astype(jnp.float32)
     else:
         ffn_vec = jnp.concatenate([grad_input_w.ravel(), grad_output_w.ravel()]) * grad_scale
         ffn_vec = ffn_vec.reshape(dp_count, ffn_piece)
@@ -568,11 +668,14 @@
     )
     grad_qkv_w = jnp.dot(grad_packed.T, full_one, preferred_element_type=jnp.float32)
     norm_one_terms = jnp.dot(grad_packed, w_qkv, preferred_element_type=jnp.float32)
-    grad_norm_one = zero_scatter(norm_one_terms.astype(jnp.bfloat16), 9)
-    gain_one_term = jnp.sum(grad_norm_one * normed_one, axis=0)
+    grad_norm_one, gain_sums = zero_scatter_gain(
+        norm_one_terms.astype(jnp.bfloat16), normed_one, gain_two_term[None], 9
+    )
+    ffn_sum, gain_sums = lax.optimization_barrier((ffn_sum, gain_sums))
+    output = hidden + ffn_sum.astype(jnp.float32)
     grad_inputs = grad_hidden + norm_backward(grad_norm_one, gain_one32, normed_one, inverse_one)
-    gain_grads = lax.psum_scatter(
-        jnp.stack([gain_one_term, gain_two_term]), "zero", scatter_dimension=1, tiled=True
+    gain_grads = lax.dynamic_slice(
+        gain_sums, (0, lax.axis_index("zero") * quarter), (2, quarter)
     )
     if aligned:
         gain_row = jnp.pad(gain_grads.reshape(1, 2 * quarter), ((0, 0), (0, D - 2 * quarter)))

time: 293 us -> 282 us (0.962)
  blocking collectives: 48.7 us -> 0 us
  waiting for transfers between devices: 0.06 us -> 32.7 us
  Pallas kernels: 129 us -> 132 us
    unnamed x1 -> x0, blocking collectives: 39.9 us -> none
    reduce_scatter x0 -> x2, waiting for transfers between devices: none -> 32.6 us  [the longest x1 32.6 us: per_device(): lax.psum_scatter(ffn_grads.reshape(dp_count * (ffn_rows + ffn_pad), D), '...]
    pallas_call x4 -> x2, Pallas kernels: 41.2 us -> 20.9 us  [zero_scatter(): pl.pallas_call(zero_scatter_kernel, out_shape=jax.ShapeDtypeStruct((rows,...]
    pallas_call x0 -> x1, Pallas kernels: none -> 15.6 us  [zero_scatter_gain(): pl.pallas_call(zero_scatter_gain_kernel, out_shape=(jax.ShapeDtypeStruct(...]
    pallas_call x1, Pallas kernels: 21.8 us -> 34.8 us  [dp_scatter(): pl.pallas_call(lambda *refs: dp_scatter_kernel(step, *refs), out_shape=ja...]
    all_gather x1 -> x0, blocking collectives: 8.86 us -> none  [per_device(): lax.all_gather(cotangent, 'zero', axis=1, tiled=True).reshape(row_count, D)]
    pallas_call x1, Pallas kernels: 34.2 us -> 30.3 us  [dp_gather(): pl.pallas_call(lambda *refs: dp_gather_kernel(tail, *refs), out_shape=(ja...]
    unnamed x2 -> x0, starting transfers between devices: 3.07 us -> none
  transfers between devices with their start and end apart: 3 -> 3, of which waited for: 0 -> 1; matrix products, arithmetic and copies ran while one was open for 28% -> 14% of each run, Pallas kernels for 30% -> 29%
where the time goes in v2:
time: 282 us; the launch traced here: 280 us
  Pallas kernels  132 us (47%)
  local copies, waits for them, and re-layouts  40.6 us (14%)
  waiting for transfers between devices  32.7 us (12%)
  other arithmetic  32.5 us (12%)
  matrix products  26.9 us (10%)
  between operations  14.9 us (5%)
    pallas_call x1, Pallas kernels, dp_scatter(): pl.pallas_call(lambda *refs: dp_scatter_kernel(step, *refs), out_shape=ja...  34.8 us
    reduce_scatter x1, waiting for transfers between devices, per_device(): lax.psum_scatter(ffn_grads.reshape(dp_count * (ffn_rows + ffn_pad), D), '...  32.6 us
    pallas_call x1, Pallas kernels, dp_gather(): pl.pallas_call(lambda *refs: dp_gather_kernel(tail, *refs), out_shape=(ja...  30.3 us
    pallas_call x3, Pallas kernels, zero_gather(): pl.pallas_call(zero_gather_kernel, out_shape=jax.ShapeDtypeStruct((zero_c...  28.9 us
    pallas_call x2, Pallas kernels, zero_scatter(): pl.pallas_call(zero_scatter_kernel, out_shape=jax.ShapeDtypeStruct((rows,...  20.9 us
    pallas_call x1, Pallas kernels, zero_scatter_gain(): pl.pallas_call(zero_scatter_gain_kernel, out_shape=(jax.ShapeDtypeStruct(...  15.6 us
    unnamed x123, local copies, waits for them, and re-layouts  8.73 us
  transfers between devices with their start and end apart: 3, of which 1 were waited for; matrix products, arithmetic and copies ran while one was open for 14% of the time, Pallas kernels for 29%

profile of v2, /device:TPU:0, one launch (start us, length us, event | category | flops | bytes accessed | tf_op | source)
XLA Modules:
  0.0 280.2 jit_solution(12091331175154278150)
XLA Ops:
  7.2 1.8 fusion.34
  9.1 1.7 slice_reduce_fusion
  12.4 1.8 shift_piece.1.refs_0_
  14.2 30.3 %dp_gather.1 = (bf16[8,112,768]{2,1,0:T(8,128)(2,1)}, bf16[4,16,768]{2,1,0:T(8,128)(2,1)}, bf16[4,128,768]{2,1,0:T(8,128)(2,1)}) custom-call(bf16[112,768]{1,0:T(8,128)(2,1)} %shift_piece.1.refs_0_, bf16[128,768]{1,0:T(8,128)(2,1)} %bitcast.189), custom_call_target="tpu_custom_call" | custom-call | tf_op jit(solution)/shard_map/dp_gather/pallas_call | solution.py:404
  51.3 9.8 %shard_map.100 = bf16[4,128,768]{2,1,0:T(8,128)(2,1)} custom-call(bf16[128,768]{1,0:T(8,128)(2,1)} %get-tuple-element.65.x_ref), custom_call_target="tpu_custom_call" | custom-call | tf_op jit(solution)/shard_map/pallas_call | solution.py:169
  61.1 2.1 convolution_bitcast_fusion
  74.9 10.4 %shard_map.101 = f32[128,768]{1,0:T(8,128)} custom-call(bf16[4,128,768]{2,1,0:T(8,128)(2,1)} %bitcast.184), custom_call_target="tpu_custom_call" | custom-call | tf_op jit(solution)/shard_map/pallas_call | solution.py:230
  87.6 9.5 %shard_map.102 = bf16[4,128,768]{2,1,0:T(8,128)(2,1)} custom-call(bf16[128,768]{1,0:T(8,128)(2,1)} %multiply_convert_fusion.3.x_ref), custom_call_target="tpu_custom_call" | custom-call | tf_op jit(solution)/shard_map/pallas_call | solution.py:169
  99.0 2.4 reshape.711
  101.3 2.9 %fusion.6 = f32[512,576]{0,1:T(8,128)} fusion(bf16[512,768]{1,0:T(8,128)(2,1)S(1)} %bitcast.176, bf16[864,768]{1,0:T(8,128)(2,1)} %reshape.711), kind=kOutput, calls=%fused_computation.28 | convolution fusion | flops 452984832 | bytes 2850816 | tf_op jit(solution)/shard_map/dot_general | solution.py:588
  104.3 1.7 reshape.687
  106.0 3.1 %fusion.16 = (bf16[512,288]{0,1:T(8,128)(2,1)S(1)}, bf16[512,288]{0,1:T(8,128)(2,1)}, bf16[512,288]{0,1:T(8,128)(2,1)S(1)}) fusion(f32[512,576]{0,1:T(8,128)} %fusion.6, bf16[512,768]{1,0:T(8,128)(2,1)} %bitcast.190, bf16[768,288]{1,0:T(8,128)(2,1)} %reshape.687), kind=kOutput, calls=%fused_computation.43 | convolution fusion | flops 228851712 | bytes 3293184 | tf_op jit(solution)/shard_map/dot_general | solution.py:601
  110.6 2.8 %fusion.70 = f32[768,288]{1,0:T(8,128)} fusion(bf16[512,768]{1,0:T(8,128)(2,1)} %bitcast.191, bf16[512,288]{0,1:T(8,128)(2,1)S(1)} %get-tuple-element.44), kind=kOutput, calls=%fused_computation.168 | convolution fusion | flops 226492416 | bytes 1966080 | tf_op jit(solution)/shard_map/dot_general | solution.py:600
  113.4 1.9 fusion.59
  115.3 1.9 pad_maximum_fusion.1
  117.2 1.8 reshape.689
  119.0 3.0 %fusion = bf16[864,768]{1,0:T(8,128)(2,1)} fusion(f32[288,768]{1,0:T(8,128)} %reshape.689, f32[576,768]{1,0:T(8,128)} %fusion.59), kind=kLoop, calls=%fused_computation.1 | loop fusion | flops 1990656 | bytes 3981312 | tf_op jit(solution)/shard_map/convert_element_type | solution.py:610
  122.0 1.6 convert_element_type.195
  125.6 1.7 convolution_convert_fusion.1
  127.3 10.5 %shard_map.103 = f32[128,768]{1,0:T(8,128)} custom-call(bf16[4,128,768]{2,1,0:T(8,128)(2,1)} %bitcast.192), custom_call_target="tpu_custom_call" | custom-call | tf_op jit(solution)/shard_map/pallas_call | solution.py:230
  137.9 1.9 multiply_reduce_fusion.1
  139.7 2.0 fusion.61
  141.7 9.6 %shard_map.104 = bf16[4,128,768]{2,1,0:T(8,128)(2,1)} custom-call(bf16[128,768]{1,0:T(8,128)(2,1)} %get-tuple-element.38.x_ref), custom_call_target="tpu_custom_call" | custom-call | tf_op jit(solution)/shard_map/pallas_call | solution.py:169
  151.3 2.3 convolution_convert_fusion.4
  153.6 1.7 reshape.692
  167.8 1.7 convolution_convert_fusion
  169.5 15.6 %shard_map.105 = (f32[128,768]{1,0:T(8,128)}, f32[8,768]{1,0:T(8,128)}) custom-call(bf16[4,128,768]{2,1,0:T(8,128)(2,1)} %bitcast.193, f32[128,768]{1,0:T(8,128)} %get-tuple-element.64.normed_ref, f32[1,768]{1,0:T(1,128)} %broadcast_in_dim.76.other_ref), custom_call_target="tpu_custom_call" | custom-call | tf_op jit(solution)/shard_map/pallas_call | solution.py:284
  186.5 1.9 add_bitcast_fusion.1
  193.3 34.8 %dp_scatter.1 = f32[112,768]{1,0:T(8,128)} custom-call(bf16[8,112,768]{2,1,0:T(8,128)(2,1)} %maximum_maximum_fusion.refs_0_), custom_call_target="tpu_custom_call" | custom-call | tf_op jit(solution)/shard_map/dp_scatter/pallas_call | solution.py:475
  229.8 32.6 %reduce-scatter.5.cloned.1.call-done = bf16[112,768]{1,0:T(8,128)(2,1)} async-done(((bf16[896,768]{1,0:T(8,128)(2,1)}), bf16[112,768]{1,0:T(8,128)(2,1)}) %reduce-scatter.5.cloned.1.call-update) | async-done | bytes 172048 | tf_op jit(solution)/shard_map/reduce_scatter | solution.py:613
  263.8 3.9 %reshape.706 = f32[1,1,156720]{2,1,0:T(1,128)} reshape(f32[156720]{0:T(1024)S(1)} %pad_maximum_fusion) | data formatting | bytes 1253760 | tf_op jit(solution)/shard_map/reshape | solution.py:704
  268.1 5.6 %multiply_subtract_fusion = (f32[1,1,156720]{2,1,0:T(1,128)}, f32[1,1,156720]{2,1,0:T(1,128)}, f32[1,1,156720]{2,1,0:T(1,128)}) fusion(f32[1,1,156720]{2,1,0:T(1,128)S(1)} %copy-done.13, f32[156720]{0:T(1024)S(1)} %copy-done.12, f32[156720]{0:T(1024)S(1)} %copy-done.11, f32[1,1,156720]{2,1,0:T(1,128)S(1)} %reshape_dynamic-update-slice_fusion, ...), kind=kLoop, calls=%fused_computation.36 | loop fusion | flops 2350800 | bytes 5641920 | tf_op jit(solution)/shard_map/sub | solution.py:718
  (237 shorter events, 49.0 us)
Async XLA Ops:
  7.2 91.8 %all-gather.3.cloned.1.call-start = ((), (), s32[]{:S(2)}) async-start(), calls=%async_computation.4 | async-start | bytes 1548288 | tf_op jit(solution)/shard_map/all_gather | solution.py:517
  44.6 144.5 %reduce-scatter.3.cloned.1.call-start = ((), (), s32[]{:S(2)}) async-start(), calls=%async_computation.2 | async-start | bytes 983040 | tf_op jit(solution)/shard_map/reduce_scatter | solution.py:593
  47.2 4.0 %copy-start.5 = (bf16[8,96,768]{2,1,0:T(8,128)(2,1)}, bf16[8,96,768]{2,1,0:T(8,128)(2,1)S(1)}, u32[]{:S(2)}) copy-start(bf16[8,96,768]{2,1,0:T(8,128)(2,1)S(1)} %select_add_fusion) | copy-start | bytes 3538948
  48.5 12.6 %copy-start.49 = (f32[128]{0:T(128)}, f32[128]{0:T(128)S(1)}, u32[]{:S(2)}) copy-start(f32[128]{0:T(128)S(1)} %broadcast_multiply_fusion.5) | copy-start | bytes 1540
  48.7 12.3 %copy-start.53 = (f32[128]{0:T(128)}, f32[128]{0:T(128)S(1)}, u32[]{:S(2)}) copy-start(f32[128]{0:T(128)S(1)} %add_rsqrt_fusion.1) | copy-start | bytes 1540
  64.5 9.1 %copy-start.8 = (bf16[768,192]{1,0:T(8,128)(2,1)}, bf16[768,192]{1,0:T(8,128)(2,1)S(1)}, u32[]{:S(2)}) copy-start(bf16[768,192]{1,0:T(8,128)(2,1)S(1)} %reshape.684) | copy-start | bytes 884740
  73.5 12.9 %copy-start.48 = (f32[4,192]{1,0:T(4,128)S(1)}, f32[4,192]{1,0:T(4,128)}, u32[]{:S(2)}) copy-start(f32[4,192]{1,0:T(4,128)} %get-tuple-element.33) | copy-start | bytes 9220
  86.5 11.2 %copy-start.51 = (f32[128]{0:T(128)}, f32[128]{0:T(128)S(1)}, u32[]{:S(2)}) copy-start(f32[128]{0:T(128)S(1)} %broadcast_multiply_fusion.4) | copy-start | bytes 1540
  86.7 11.0 %copy-start.55 = (f32[128]{0:T(128)}, f32[128]{0:T(128)S(1)}, u32[]{:S(2)}) copy-start(f32[128]{0:T(128)S(1)} %add_rsqrt_fusion) | copy-start | bytes 1540
  99.0 2.4 copy-start.2
  101.3 2.9 %slice-start = ((bf16[864,768]{1,0:T(8,128)(2,1)}), bf16[288,768]{1,0:T(8,128)(2,1)S(1)}, s32[]{:S(2)}) async-start(bf16[864,768]{1,0:T(8,128)(2,1)} %reshape.711), calls=%async_computation.5 | async-start | bytes 884736 | tf_op jit(solution)/shard_map/slice | solution.py:528
  106.0 3.1 %copy-start.14 = (bf16[768,288]{1,0:T(8,128)(2,1)S(1)}, bf16[768,288]{1,0:T(8,128)(2,1)}, u32[]{:S(2)}) copy-start(bf16[768,288]{1,0:T(8,128)(2,1)} %reshape.687) | copy-start | bytes 1327108
  109.1 4.3 %copy-start.24 = (bf16[512,288]{0,1:T(8,128)(2,1)}, bf16[512,288]{0,1:T(8,128)(2,1)S(1)}, u32[]{:S(2)}) copy-start(bf16[512,288]{0,1:T(8,128)(2,1)S(1)} %get-tuple-element.42) | copy-start | bytes 884740
  110.6 2.8 %copy-start.25 = (bf16[512,288]{0,1:T(8,128)(2,1)S(1)}, bf16[512,288]{0,1:T(8,128)(2,1)}, u32[]{:S(2)}) copy-start(bf16[512,288]{0,1:T(8,128)(2,1)} %get-tuple-element.43) | copy-start | bytes 884740
  125.6 12.2 %copy-start.52 = (f32[128]{0:T(128)S(1)}, f32[128]{0:T(128)}, u32[]{:S(2)}) copy-start(f32[128]{0:T(128)} %copy-done.51) | copy-start | bytes 1540
  125.6 12.2 %copy-start.56 = (f32[128]{0:T(128)S(1)}, f32[128]{0:T(128)}, u32[]{:S(2)}) copy-start(f32[128]{0:T(128)} %copy-done.55) | copy-start | bytes 1540
  127.3 12.4 %copy-start.32 = (bf16[1,128,768]{2,1,0:T(8,128)(2,1)S(1)}, bf16[1,128,768]{2,1,0:T(8,128)(2,1)}, u32[]{:S(2)}) copy-start(bf16[1,128,768]{2,1,0:T(8,128)(2,1)} %param.6) | copy-start | bytes 589828
  137.8 13.5 %copy-start.9 = (bf16[768,192]{1,0:T(8,128)(2,1)S(1)}, bf16[768,192]{1,0:T(8,128)(2,1)}, u32[]{:S(2)}) copy-start(bf16[768,192]{1,0:T(8,128)(2,1)} %copy-done.8) | copy-start | bytes 884740
  141.7 14.6 %copy-start.22 = (bf16[1,4,128,3,64]{2,1,4,3,0:T(4,128)(2,1)S(1)}, bf16[1,4,128,3,64]{2,1,4,3,0:T(4,128)(2,1)}, u32[]{:S(2)}) copy-start(bf16[1,4,128,3,64]{2,1,4,3,0:T(4,128)(2,1)} %copy-done.21) | copy-start | bytes 589828
  151.3 5.0 %copy-start = (bf16[4,128,768]{2,1,0:T(8,128)(2,1)S(1)}, bf16[4,128,768]{2,1,0:T(8,128)(2,1)}, u32[]{:S(2)}) copy-start(bf16[4,128,768]{2,1,0:T(8,128)(2,1)} %shard_map.104) | copy-start | bytes 2359300
  157.7 104.7 %reduce-scatter.5.cloned.1.call-start = ((), (), s32[]{:S(2)}) async-start(), calls=%async_computation.3 | async-start | bytes 1548288 | tf_op jit(solution)/shard_map/reduce_scatter | solution.py:613
  167.8 17.4 %copy-start.50 = (f32[128]{0:T(128)S(1)}, f32[128]{0:T(128)}, u32[]{:S(2)}) copy-start(f32[128]{0:T(128)} %copy-done.49) | copy-start | bytes 1540
  167.8 17.4 %copy-start.54 = (f32[128]{0:T(128)S(1)}, f32[128]{0:T(128)}, u32[]{:S(2)}) copy-start(f32[128]{0:T(128)} %copy-done.53) | copy-start | bytes 1540
  169.5 16.9 %copy-start.23 = (f32[128,768]{1,0:T(8,128)S(1)}, f32[128,768]{1,0:T(8,128)}, u32[]{:S(2)}) copy-start(f32[128,768]{1,0:T(8,128)} %get-tuple-element.39) | copy-start | bytes 1179652
  169.5 18.9 %copy-start.1 = (bf16[4,128,768]{2,1,0:T(8,128)(2,1)S(1)}, bf16[4,128,768]{2,1,0:T(8,128)(2,1)}, u32[]{:S(2)}) copy-start(bf16[4,128,768]{2,1,0:T(8,128)(2,1)} %shard_map.100) | copy-start | bytes 2359300
  185.2 3.3 %copy-start.16 = (bf16[1,512,3,3,64]{1,4,3,2,0:T(8,128)(2,1)S(1)}, bf16[1,512,3,3,64]{1,4,3,2,0:T(8,128)(2,1)}, u32[]{:S(2)}) copy-start(bf16[1,512,3,3,64]{1,4,3,2,0:T(8,128)(2,1)} %copy-done.15) | copy-start | bytes 1769476
  193.3 35.8 %copy-start.46 = (bf16[128,768]{1,0:T(8,128)(2,1)S(1)}, bf16[128,768]{1,0:T(8,128)(2,1)}, u32[]{:S(2)}) copy-start(bf16[128,768]{1,0:T(8,128)(2,1)} %reduce-scatter.3.cloned.1.call-done) | copy-start | bytes 589828
  263.7 4.3 %copy-start.44 = (f32[1,1,156720]{2,1,0:T(1,128)S(1)}, f32[1,1,156720]{2,1,0:T(1,128)}, u32[]{:S(2)}) copy-start(f32[1,1,156720]{2,1,0:T(1,128)} %param.9) | copy-start | bytes 1880644
  263.8 4.2 %copy-start.11 = (f32[156720]{0:T(1024)S(1)}, f32[156720]{0:T(1024)}, u32[]{:S(2)}) copy-start(f32[156720]{0:T(1024)} %get-tuple-element.68) | copy-start | bytes 1880644
  263.8 4.2 %copy-start.12 = (f32[156720]{0:T(1024)S(1)}, f32[156720]{0:T(1024)}, u32[]{:S(2)}) copy-start(f32[156720]{0:T(1024)} %get-tuple-element.69) | copy-start | bytes 1880644
  263.8 4.2 %copy-start.13 = (f32[1,1,156720]{2,1,0:T(1,128)S(1)}, f32[1,1,156720]{2,1,0:T(1,128)}, u32[]{:S(2)}) copy-start(f32[1,1,156720]{2,1,0:T(1,128)} %param.7) | copy-start | bytes 1880644
  263.8 4.2 %copy-start.43 = (f32[1,1,156720]{2,1,0:T(1,128)S(1)}, f32[1,1,156720]{2,1,0:T(1,128)}, u32[]{:S(2)}) copy-start(f32[1,1,156720]{2,1,0:T(1,128)} %param.8) | copy-start | bytes 1880644
  (31 other events, 39.6 us)
Sparse Core Ops, SparseCore 0:
  44.7 44.6 all-gather.2
  157.8 27.4 reduce-scatter.2
  188.7 73.5 reduce-scatter.4
